TPU v7x, 32 devices: a whole 2x2x4 slice. The times are simulated.
32 devices in a mesh: enc: 8 (over z, y), slide: 4 (over x, core).
Axes of the slice: x: 2, y: 2, z: 4, core: 2. Of those that a mesh axis runs over, the one named last changes fastest.
Arguments:
- tile_features: bfloat16 [512, 7, 7, 768], P(('enc', 'slide')), may hold values from -6 to 6
- tile_slide: int32 [512, 1], P(('enc', 'slide')), may hold values from 0 to 7, as said below
- slide_order: int32 [8, 8], P('enc'), may hold values from 0 to 7, each once within a row
- targets: float32 [8, 8, 256], P('enc', 'slide'), may hold values from -6 to 6
- dw_kernel: bfloat16 [49, 768], replicated, may hold values from -0.875 to 0.875
- dw_bias: bfloat16 [768], replicated, may hold values from -3 to 3
- norm_gain: bfloat16 [768], replicated, may hold values from 0.25 to 1.75
- norm_bias: bfloat16 [768], replicated, may hold values from -3 to 3
- w_in: bfloat16 [3072, 768], replicated, may hold values from -0.21875 to 0.21875
- in_bias: bfloat16 [3072], replicated, may hold values from -3 to 3
- w_out: bfloat16 [3072, 768], replicated, may hold values from -0.109375 to 0.109375
- out_bias: bfloat16 [768], replicated, may hold values from -3 to 3
- layer_scale: bfloat16 [768], replicated, may hold values from 0.19921875 to 2
- final_gain: bfloat16 [768], replicated, may hold values from 0.25 to 1.75
- final_bias: bfloat16 [768], replicated, may hold values from -3 to 3
- head_weight: bfloat16 [768, 256], replicated, may hold values from -0.21875 to 0.21875
- head_bias: bfloat16 [256], replicated, may hold values from -3 to 3
Outputs:
- grad_w_in: float32 [3072, 768], P(('enc', 'slide'))
- grad_w_out: float32 [3072, 768], P(('enc', 'slide'))
- grad_dw_kernel: float32 [49, 768], replicated
- grad_vectors: float32 [7, 768], replicated
- grad_in_bias: float32 [3072], replicated
- grad_head_weight: float32 [768, 256], replicated
- grad_head_bias: float32 [256], replicated
- slide_loss: float32 [8, 8], P('enc', 'slide')
Inputs may be any that keep to these rules, and one draw needn't show every extreme that they name: `tile_slide`: the 16 tiles of one device are the rows of one aligned block; at most 3 tiles of one device belong to one slide, and every device has exactly 3 tiles of some slide; a slide may have no tiles in its group. `slide_order`: each row names every slide number of its group once.
All inputs are finite; a program needn't handle non-finite values.
Results may differ from a plain program's by a relative error of at most 0.0041.
Values may be sent and summed in bfloat16 or wider, within the bound.
A program may use at most 192 MiB of HBM per device.

v0:
```python
from functools import partial

import jax
import jax.numpy as jnp
from jax import lax
from jax.sharding import PartitionSpec as P

KERNEL = 7
SIDE = 7


epsilon = 1e-06


def layer_norm(values, gain, shift):
    center = values - jnp.mean(values, axis=-1, keepdims=True)
    spread = jnp.mean(center * center, axis=-1, keepdims=True)
    return center * lax.rsqrt(spread + epsilon) * gain + shift


def depthwise(features, kernel, bias):
    margin = KERNEL // 2
    padded = jnp.pad(
        features.astype(jnp.float32), ((0, 0), (margin, margin), (margin, margin), (0, 0))
    )
    total = jnp.zeros(features.shape, jnp.float32) + bias
    for vertical in range(KERNEL):
        for across in range(KERNEL):
            total = (
                total
                + padded[:, vertical : vertical + SIDE, across : across + SIDE, :]
                * kernel[vertical * KERNEL + across]
            )
    return total


def prepare_tile(features, kernel, dw_bias, norm_gain, norm_bias):
    conv = depthwise(features, kernel, dw_bias)
    return layer_norm(conv, norm_gain, norm_bias).reshape(-1, features.shape[-1])


def finish_tile(projected, out_bias, layer_scale, final_gain, final_bias, features):
    tile_count = features.shape[0]
    channels = features.shape[-1]
    branch = (projected + out_bias).reshape(tile_count, -1, channels)
    summed = features.astype(jnp.float32).reshape(tile_count, -1, channels) + layer_scale * branch
    pooled = jnp.mean(summed, axis=1)
    return layer_norm(pooled, final_gain, final_bias)


def contract_rows(left, right):
    return lax.dot_general(
        left, right, (((0,), (0,)), ((), ())), preferred_element_type=jnp.float32
    )


def encode(features, vector_params, w_in, inner_bias, w_out):
    kernel, dw_bias, norm_gain, norm_bias, out_bias, layer_scale, final_gain, final_bias = (
        vector_params
    )
    normed = prepare_tile(features, kernel, dw_bias, norm_gain, norm_bias).astype(jnp.bfloat16)
    hidden = (
        lax.dot_general(normed, w_in, (((1,), (1,)), ((), ())), preferred_element_type=jnp.float32)
        + inner_bias
    )
    active = jax.nn.gelu(hidden, approximate=False).astype(jnp.bfloat16)
    projected = jnp.dot(active, w_out, preferred_element_type=jnp.float32)
    embedded = finish_tile(
        projected, out_bias, layer_scale, final_gain, final_bias, features
    ).astype(jnp.bfloat16)
    return (embedded, (normed, hidden, active, projected))


def decode(features, vector_params, w_in, w_out, stored, grad_embed):
    kernel, dw_bias, norm_gain, norm_bias, out_bias, layer_scale, final_gain, final_bias = (
        vector_params
    )
    normed, hidden, active, projected = stored
    unused, pull_finish = jax.vjp(
        partial(finish_tile, features=features),
        projected,
        out_bias,
        layer_scale,
        final_gain,
        final_bias,
    )
    grad_proj, grad_out_bias, grad_scale, grad_fgain, grad_fbias = pull_finish(
        grad_embed.astype(jnp.float32)
    )
    grad_projected = grad_proj.astype(jnp.bfloat16)
    grad_active = lax.dot_general(
        grad_projected, w_out, (((1,), (1,)), ((), ())), preferred_element_type=jnp.float32
    )
    unused_gelu, pull_gelu = jax.vjp(partial(jax.nn.gelu, approximate=False), hidden)
    grad_wide = pull_gelu(grad_active)[0]
    grad_hidden = grad_wide.astype(jnp.bfloat16)
    grad_normed = jnp.dot(grad_hidden, w_in, preferred_element_type=jnp.float32)
    unused_prep, pull_prepare = jax.vjp(
        partial(prepare_tile, features), kernel, dw_bias, norm_gain, norm_bias
    )
    grad_kernel, grad_dw_bias, grad_ngain, grad_nbias = pull_prepare(grad_normed)
    vectors = jnp.stack(
        [grad_dw_bias, grad_ngain, grad_nbias, grad_out_bias, grad_scale, grad_fgain, grad_fbias]
    )
    return (grad_projected, grad_hidden, grad_kernel, vectors, jnp.sum(grad_wide, axis=0))


def per_device(
    tile_features,
    tile_slide,
    slide_order,
    targets,
    dw_kernel,
    dw_bias,
    norm_gain,
    norm_bias,
    w_in,
    in_bias,
    w_out,
    out_bias,
    layer_scale,
    final_gain,
    final_bias,
    head_weight,
    head_bias,
):
    highest = lax.Precision.HIGHEST
    channels = tile_features.shape[-1]
    tile_count = tile_features.shape[0]
    n_slide = lax.axis_size("slide")
    group_slides = slide_order.shape[1]
    per_owner = group_slides // n_slide
    capacity = max(2, -(-tile_count // (group_slides - 1)))
    vector_params = tuple(
        (
            param.astype(jnp.float32)
            for param in (
                dw_kernel,
                dw_bias,
                norm_gain,
                norm_bias,
                out_bias,
                layer_scale,
                final_gain,
                final_bias,
            )
        )
    )
    embedded, stored = encode(
        tile_features, vector_params, w_in, in_bias.astype(jnp.float32), w_out
    )
    slide_ids = tile_slide[:, 0]
    positions = jnp.arange(group_slides, dtype=jnp.int32)
    order_match = slide_order[0][None, :] == positions[:, None]
    position_of = jnp.sum(jnp.where(order_match, positions[None, :], 0), axis=1)
    tile_match = slide_ids[:, None] == positions[None, :]
    tile_position = jnp.sum(jnp.where(tile_match, position_of[None, :], 0), axis=1)
    position_hot = (tile_position[:, None] == positions[None, :]).astype(jnp.bfloat16)
    tile_index = jnp.arange(tile_count, dtype=jnp.int32)
    same_place = tile_position[:, None] == tile_position[None, :]
    earlier = tile_index[None, :] < tile_index[:, None]
    arrival = jnp.sum((same_place & earlier).astype(jnp.int32), axis=1)
    slot_number = tile_position * capacity + arrival
    slot_range = jnp.arange(group_slides * capacity, dtype=jnp.int32)
    slot_hot = (slot_range[:, None] == slot_number[None, :]).astype(jnp.bfloat16)
    outgoing = jnp.dot(slot_hot, embedded, preferred_element_type=jnp.float32).astype(jnp.bfloat16)
    outgoing = outgoing.reshape(n_slide, per_owner * capacity, channels)
    local_counts = (
        jnp.sum(position_hot.astype(jnp.float32), axis=0)
        .astype(jnp.bfloat16)
        .reshape(n_slide, per_owner)
    )
    incoming, incoming_counts = (
        lax.all_to_all(outgoing, "slide", split_axis=0, concat_axis=0, tiled=True),
        lax.all_to_all(local_counts, "slide", split_axis=0, concat_axis=0, tiled=True),
    )
    slide_sums = jnp.sum(
        incoming.astype(jnp.float32).reshape(n_slide, per_owner, capacity, channels), axis=(0, 2)
    )
    slide_counts = jnp.sum(incoming_counts.astype(jnp.float32), axis=0)
    divisor = jnp.maximum(slide_counts, 1.0)[:, None]
    slide_mean = slide_sums / divisor
    head_wide = head_weight.astype(jnp.float32)
    prediction = jnp.dot(
        slide_mean, head_wide, precision=highest, preferred_element_type=jnp.float32
    ) + head_bias.astype(jnp.float32)
    difference = prediction - targets[0]
    slide_loss = 0.5 * jnp.mean(difference * difference, axis=-1)
    grad_pred = difference / difference.shape[-1]
    grad_head_w = jnp.dot(
        slide_mean.T, grad_pred, precision=highest, preferred_element_type=jnp.float32
    )
    grad_head_b = jnp.sum(grad_pred, axis=0)
    grad_mean = jnp.dot(
        grad_pred, head_wide.T, precision=highest, preferred_element_type=jnp.float32
    )
    slide_grad = (grad_mean / divisor).astype(jnp.bfloat16)
    spread_grads = jnp.broadcast_to(
        slide_grad[None, :, None, :], (n_slide, per_owner, capacity, channels)
    )
    spread_grads = spread_grads.reshape(n_slide, per_owner * capacity, channels)
    returned = lax.all_to_all(
        spread_grads, "slide", split_axis=0, concat_axis=0, tiled=True
    ).reshape(group_slides * capacity, channels)
    grad_embed = contract_rows(slot_hot, returned).astype(jnp.bfloat16)
    grad_projected, grad_hidden, grad_kernel, grad_vectors, grad_inner = decode(
        tile_features, vector_params, w_in, w_out, stored, grad_embed
    )
    normed, hidden, active, projected = stored
    stacked = lax.psum_scatter(
        jnp.concatenate(
            [contract_rows(grad_hidden, normed), contract_rows(active, grad_projected)], axis=1
        ),
        ("enc", "slide"),
        scatter_dimension=0,
        tiled=True,
    )
    grad_w_in = stacked[:, :channels]
    grad_w_out = stacked[:, channels:]
    totals = lax.psum(
        (grad_kernel, grad_vectors, grad_inner, grad_head_w, grad_head_b), ("enc", "slide")
    )
    return (
        grad_w_in,
        grad_w_out,
        totals[0],
        totals[1],
        totals[2],
        totals[3],
        totals[4],
        slide_loss[None, :],
    )


def solution(mesh):
    placed = (
        P(("enc", "slide"), None, None, None),
        P(("enc", "slide"), None),
        P("enc", None),
        P("enc", "slide", None),
        P(),
        P(),
        P(),
        P(),
        P(),
        P(),
        P(),
        P(),
        P(),
        P(),
        P(),
        P(),
        P(),
    )
    return jax.shard_map(
        per_device,
        mesh=mesh,
        in_specs=placed,
        out_specs=(
            P(("enc", "slide"), None),
            P(("enc", "slide"), None),
            P(),
            P(),
            P(),
            P(),
            P(),
            P("enc", "slide"),
        ),
        check_vma=False,
    )
```

profile of v0, /device:TPU:0, one launch (start us, length us, event | category | flops | bytes accessed | tf_op | source)
XLA Modules:
  0.0 508.9 jit_solution(8024968280926762521)
XLA Ops:
  7.2 0.9 select_reduce_fusion.1
  8.1 0.7 select_reduce_fusion
  9.0 0.7 all_to_all.16
  9.6 4.2 all-to-all-start.1
  13.8 0.9 convert_element_type.88
  15.2 0.7 convert_reduce_fusion.1
  15.9 1.7 copy_convert_fusion
  17.6 17.5 %fusion.39 = (f32[16,7,7]{2,1,0:T(8,128)S(1)}, f32[16,7,7,768]{3,2,1,0:T(8,128)S(1)}) fusion(f32[768]{0:T(1024)S(1)} %get-tuple-element.105, f32[768]{0:T(1024)S(1)} %get-tuple-element.106, f32[768]{0:T(1024)S(1)} %get-tuple-element.107, f32[768]{0:T(1024)S(1)} %get-tuple-element.108, f32[768]{0:T(1024)S(1)} %get-tuple-element.109, ...), kind=kLoop, calls=%fused_computation.246 | loop fusion | flops 60210416 | bytes 6177856 | tf_op jit(solution)/shard_map/reduce_sum | solution.py:16
  35.2 0.5 multiply_reduce_fusion.52
  35.9 0.9 copy-done.17
  36.8 0.6 copy-done.19
  37.4 0.5 add_convert_fusion
  37.8 0.4 convert_element_type.92
  38.4 27.6 %multiply_convert_fusion = (bf16[784,3072]{1,0:T(8,128)(2,1)S(1)}, f32[784,3072]{1,0:T(8,128)}, f32[784,3072]{1,0:T(8,128)}) fusion(f32[3072]{0:T(1024)S(1)} %convert_element_type.93, bf16[784,768]{1,0:T(8,128)(2,1)S(1)} %convert_element_type.92, bf16[3072,768]{1,0:T(8,128)(2,1)} %param.25), kind=kOutput, calls=%fused_computation.52 | convolution fusion | flops 3858333696 | bytes 30019584 | tf_op jit(solution)/shard_map/dot_general | solution.py:63
  66.0 2.2 copy-done.34
  68.2 7.6 %convolution_add_fusion = f32[784,768]{1,0:T(8,128)} fusion(bf16[784,3072]{1,0:T(8,128)(2,1)S(1)} %get-tuple-element.166, bf16[3072,768]{1,0:T(8,128)(2,1)} %param.27, f32[768]{0:T(1024)S(1)} %convert_element_type.97), kind=kOutput, calls=%fused_computation.129 | convolution fusion | flops 3699978240 | bytes 11947008 | tf_op jit(solution)/shard_map/dot_general | solution.py:67
  75.8 3.5 reshape.405
  79.4 2.5 add_reduce_fusion
  82.6 0.6 reshape.406
  83.2 4.0 all-to-all-start
  87.2 0.7 convert_reduce_fusion.2
  87.9 3.3 all-to-all-done
  91.3 0.4 multiply_reduce_fusion.58
  92.3 6.4 %all_to_all.20 = bf16[4,6,768]{2,1,0:T(8,128)(2,1)S(1)} all-to-all(bf16[4,6,768]{2,1,0:T(8,128)(2,1)S(1)} %broadcast_in_dim.240), channel_id=1, replica_groups=mesh['enc'=8,'slide'=4] {'slide'}, dimensions={0} | all-to-all | bytes 73728 | tf_op jit(solution)/shard_map/all_to_all | solution.py:202
  99.5 1.6 broadcast_in_dim.244
  101.1 8.3 %fusion.13 = f32[3072,768]{0,1:T(8,128)S(1)} fusion(bf16[784,3072]{1,0:T(8,128)(2,1)} %copy-done.34, f32[784,768]{1,0:T(8,128)} %broadcast_in_dim.244, f32[768]{0:T(1024)S(1)} %convert_element_type.94), kind=kOutput, calls=%fused_computation.139 | convolution fusion | flops 3700580352 | bytes 16665600 | tf_op jit(solution)/shard_map/dot_general | solution.py:52
  109.4 13.4 %fusion.42 = (f32[3072]{0:T(1024)S(1)}, bf16[784,3072]{1,0:T(8,128)(2,1)}) fusion(f32[784,3072]{1,0:T(8,128)} %get-tuple-element.167, bf16[3072,768]{1,0:T(8,128)(2,1)} %param.27, f32[784,768]{1,0:T(8,128)S(1)} %copy-done.10, f32[768]{0:T(1024)S(1)} %convert_element_type.94, f32[784,3072]{1,0:T(8,128)} %get-tuple-element.172, ...), kind=kOutput, calls=%fused_computation.249 | convolution fusion | flops 3739112448 | bytes 31239168 | tf_op jit(solution)/shard_map/dot_general | solution.py:91
  122.8 7.1 %fusion.8 = f32[3072,768]{0,1:T(8,128)S(1)} fusion(bf16[784,768]{1,0:T(8,128)(2,1)S(1)} %copy-done.14, bf16[784,3072]{1,0:T(8,128)(2,1)} %get-tuple-element.177), kind=kOutput, calls=%fused_computation.126 | convolution fusion | flops 3699376128 | bytes 15458304 | tf_op jit(solution)/shard_map/dot_general | solution.py:52
  130.0 7.3 %pad_maximum_fusion = f32[3072,1536]{0,1:T(8,128)} fusion(f32[3072,768]{0,1:T(8,128)S(1)} %fusion.13, f32[3072,768]{0,1:T(8,128)S(1)} %fusion.8), kind=kLoop, calls=%fused_computation.48 | loop fusion | flops 4718592 | bytes 37748736 | tf_op jit(solution)/shard_map/concatenate | solution.py:211
  137.3 18.7 %copy.41 = f32[3072,1536]{1,0:T(8,128)} copy(f32[3072,1536]{0,1:T(8,128)} %pad_maximum_fusion) | data formatting | bytes 37748736
  156.2 0.5 multiply_bitcast_fusion
  156.7 1.8 fusion.27
  158.5 9.1 %fusion.41 = (f32[768]{0:T(1024)S(1)}, f32[784,768]{1,0:T(8,128)}) fusion(bf16[3072,768]{1,0:T(8,128)(2,1)} %param.25, bf16[784,3072]{1,0:T(8,128)(2,1)} %get-tuple-element.177), kind=kOutput, calls=%fused_computation.248 | convolution fusion | flops 3699977472 | bytes 11947008 | tf_op jit(solution)/shard_map/dot_general | solution.py:97
  167.7 4.6 reshape.408
  172.3 2.9 multiply_reduce_fusion.51
  175.4 1.5 multiply_reduce_fusion.1
  176.9 0.4 copy-done.4
  177.8 6.6 %fusion.36 = (f32[768]{0:T(1024)S(1)}, f32[768]{0:T(1024)S(1)}, f32[768]{0:T(1024)S(1)}, f32[768]{0:T(1024)S(1)}, f32[768]{0:T(1024)S(1)}, /*index=5*/f32[768]{0...) fusion(bf16[16,7,7,768]{3,0,2,1:T(8,128)(2,1)S(1)} %copy-done.8, ...), kind=kLoop, calls=%fused_computation.244 | loop fusion | flops 21063168 | bytes 10896640 | tf_op jit(solution)/shard_map/transpose(jvp())/reduce_sum | solution.py:26
  184.4 8.0 %multiply_reduce_fusion.49 = (f32[768]{0:T(1024)S(1)}, f32[768]{0:T(1024)S(1)}, f32[768]{0:T(1024)S(1)}, f32[768]{0:T(1024)S(1)}, f32[768]{0:T(1024)S(1)}, /*ind...) fusion(f32[16,7,7,768]{3,2,1,0:T(8,128)S(1)} %get-tuple-element, ...), kind=kLoop, calls=%fused_computation.116 | loop fusion | flops 21662208 | bytes 4872192 | tf_op jit(solution)/shard_map/transpose(jvp())/reduce_sum | solution.py:31
  192.7 6.9 %multiply_reduce_fusion.50 = (f32[768]{0:T(1024)S(1)}, f32[768]{0:T(1024)S(1)}, f32[768]{0:T(1024)S(1)}, f32[768]{0:T(1024)S(1)}, f32[768]{0:T(1024)S(1)}, /*ind...) fusion(f32[16,7,7,768]{3,2,1,0:T(8,128)S(1)} %get-tuple-element, ...), kind=kLoop, calls=%fused_computation.117 | loop fusion | flops 21662208 | bytes 4872192 | tf_op jit(solution)/shard_map/transpose(jvp())/reduce_sum | solution.py:31
  200.0 1.0 pad_add_fusion
  201.0 2.2 multiply_reduce_fusion.53
  203.5 43.6 %all-reduce.50 = (f32[7,768]{1,0:T(8,128)}, f32[3072]{0:T(1024)}, f32[256]{0:T(256)}) all-reduce(f32[7,768]{1,0:T(8,128)S(1)} %stack.22, f32[3072]{0:T(1024)S(1)} %get-tuple-element.176, f32[256]{0:T(256)S(1)} %get-tuple-element.157), channel_id=1, replica_groups=mesh['enc'=8,'slide'=4] {'enc','slide'}, use_global_device_ids=true, to_apply=%region_74.75 | all-reduce | flops 8704 | bytes 69632 | tf_op jit(solution)/shard_map/psum | solution.py:220
  247.1 117.6 %reduce-scatter.4.cloned.1.call-done = f32[96,1536]{1,0:T(8,128)} async-done(((f32[3072,1536]{1,0:T(8,128)}), f32[96,1536]{1,0:T(8,128)}) %reduce-scatter.4.cloned.1.call-update) | async-done | bytes 589840
  364.7 1.9 fusion.40
  366.6 131.8 %all-reduce.54.cloned.1.call-done = (f32[49,768]{1,0:T(8,128)}, f32[768,256]{1,0:T(8,128)}) async-done(((f32[49,768]{1,0:T(8,128)}, f32[768,256]{1,0:T(8,128)}), (f32[49,768]{1,0:T(8,128)}, f32[768,256]{1,0:T(8,128)})) %all-reduce.54.cloned.1.call-update) | async-done | bytes 936976 | tf_op jit(solution)/shard_map/psum | solution.py:220
  498.4 1.6 copy.52
  500.0 2.1 copy.53
  (167 shorter events, 4.1 us)
Async XLA Ops:
  7.2 84.1 %copy-start = (bf16[768,256]{1,0:T(8,128)(2,1)S(1)}, bf16[768,256]{1,0:T(8,128)(2,1)}, u32[]{:S(2)}) copy-start(bf16[768,256]{1,0:T(8,128)(2,1)} %param.32) | copy-start | bytes 1179652
  7.2 10.4 %copy-start.6 = (bf16[16,7,7,768]{3,0,2,1:T(8,128)(2,1)S(1)}, bf16[16,7,7,768]{3,0,2,1:T(8,128)(2,1)}, u32[]{:S(2)}) copy-start(bf16[16,7,7,768]{3,0,2,1:T(8,128)(2,1)} %param.17) | copy-start | bytes 3612676
  7.2 10.4 %copy-start.22 = (bf16[768]{0:T(1024)(128)(2,1)S(1)}, bf16[768]{0:T(1024)(128)(2,1)}, u32[]{:S(2)}) copy-start(bf16[768]{0:T(1024)(128)(2,1)} %param.22) | copy-start | bytes 4612
  8.8 26.3 %copy-start.31 = (s32[16]{0:T(128)}, s32[16]{0:T(128)S(1)}, u32[]{:S(2)}) copy-start(s32[16]{0:T(128)S(1)} %select_reduce_fusion) | copy-start | bytes 196
  9.6 73.6 %all-to-all-start.1 = ((bf16[4,1,2]{2,1,0:T(2,128)(2,1)}), bf16[4,1,2]{2,1,0:T(2,128)(2,1)}, u32[]{:S(2)}, u32[]{:S(2)}) async-start(bf16[4,1,2]{2,1,0:T(2,128)(2,1)} %all_to_all.16), calls=%async_computation.1 | async-start | bytes 4096 | tf_op jit(solution)/shard_map/all_to_all | solution.py:175
  17.6 17.5 %copy-start.3 = (f32[16,7,7,768]{3,2,1,0:T(8,128)}, f32[16,7,7,768]{3,2,1,0:T(8,128)S(1)}, u32[]{:S(2)}) copy-start(f32[16,7,7,768]{3,2,1,0:T(8,128)S(1)} %copy_convert_fusion) | copy-start | bytes 7225348
  35.1 1.6 copy-start.1
  35.1 0.7 copy-start.23
  35.2 1.6 copy-start.24
  35.2 1.6 copy-start.11
  35.7 1.0 copy-start.17
  35.9 0.9 copy-start.15
  36.8 0.6 copy-start.19
  37.3 1.0 copy-start.21
  37.3 1.0 copy-start.25
  38.3 27.7 %copy-start.13 = (bf16[784,768]{1,0:T(8,128)(2,1)}, bf16[784,768]{1,0:T(8,128)(2,1)S(1)}, u32[]{:S(2)}) copy-start(bf16[784,768]{1,0:T(8,128)(2,1)S(1)} %convert_element_type.92) | copy-start | bytes 3612676
  66.0 2.2 copy-start.34
  75.8 3.5 copy-start.26
  75.8 3.6 copy-start.7
  79.4 2.9 copy-start.32
  79.4 2.9 copy-start.33
  79.4 3.0 copy-start.27
  79.4 3.0 copy-start.28
  79.4 3.8 copy-start.30
  79.4 11.9 %copy-start.29 = (f32[1,2,256]{2,1,0:T(2,128)S(1)}, f32[1,2,256]{2,1,0:T(2,128)}, u32[]{:S(2)}) copy-start(f32[1,2,256]{2,1,0:T(2,128)} %param.20) | copy-start | bytes 6148
  83.2 8.0 %all-to-all-start = ((bf16[4,6,768]{2,1,0:T(8,128)(2,1)}), bf16[4,6,768]{2,1,0:T(8,128)(2,1)S(1)}, u32[]{:S(2)}, u32[]{:S(2)}) async-start(bf16[4,6,768]{2,1,0:T(8,128)(2,1)} %reshape.406), calls=%async_computation | async-start | bytes 98304 | tf_op jit(solution)/shard_map/all_to_all | solution.py:174
  87.2 277.5 %reduce-scatter.4.cloned.1.call-start = ((), (), s32[]{:S(2)}) async-start(), calls=%async_computation.4 | async-start | bytes 19464192
  101.1 8.3 %copy-start.10 = (f32[784,768]{1,0:T(8,128)S(1)}, f32[784,768]{1,0:T(8,128)}, u32[]{:S(2)}) copy-start(f32[784,768]{1,0:T(8,128)} %broadcast_in_dim.244) | copy-start | bytes 7225348
  109.4 13.4 %copy-start.14 = (bf16[784,768]{1,0:T(8,128)(2,1)S(1)}, bf16[784,768]{1,0:T(8,128)(2,1)}, u32[]{:S(2)}) copy-start(bf16[784,768]{1,0:T(8,128)(2,1)} %copy-done.13) | copy-start | bytes 3612676
  156.0 342.4 %all-reduce.54.cloned.1.call-start = ((), (), s32[]{:S(2)}) async-start(), calls=%async_computation.5 | async-start | bytes 1916928 | tf_op jit(solution)/shard_map/psum | solution.py:220
  167.7 4.6 copy-start.2
  167.7 4.6 copy-start.12
  167.7 4.6 copy-start.20
  172.3 2.9 copy-start.18
  172.3 3.1 copy-start.5
  172.3 3.1 copy-start.16
  175.4 2.0 copy-start.4
  175.4 2.5 copy-start.8
  192.7 8.4 %copy-start.9 = (f32[784,768]{1,0:T(8,128)S(1)}, f32[784,768]{1,0:T(8,128)}, u32[]{:S(2)}) copy-start(f32[784,768]{1,0:T(8,128)} %convolution_add_fusion) | copy-start | bytes 7225348
Sparse Core Ops, SparseCore 0:
  156.1 208.5 reduce-scatter.3
  370.5 127.8 all-reduce.53
where the time goes:
time: 510 us; the launch traced here: 509 us
  waiting for transfers between devices  253 us (50%)
  matrix products  76.4 us (15%)
  other arithmetic  64.7 us (13%)
  blocking collectives  50 us (10%)
  local copies, waits for them, and re-layouts  41.7 us (8%)
  between operations  15 us (3%)
  starting transfers between devices  8.43 us (2%)
    psum x1, waiting for transfers between devices, per_device(): lax.psum((grad_kernel, grad_vectors, grad_inner, grad_head_w, grad_head_b...  132 us
    unnamed x3, waiting for transfers between devices  118 us
    psum x1, blocking collectives, per_device(): lax.psum((grad_kernel, grad_vectors, grad_inner, grad_head_w, grad_head_b...  43.6 us
    dot_general x1, matrix products, encode(): lax.dot_general(normed, w_in, (((1,), (1,)), ((), ())), preferred_element...  27.6 us
    unnamed x73, local copies, waits for them, and re-layouts  27.3 us
    reduce_sum x3, other arithmetic, layer_norm(): center = values - jnp.mean(values, axis=-1, keepdims=True)  17.8 us
    dot_general x3, matrix products, contract_rows(): lax.dot_general(left, right, (((0,), (0,)), ((), ())), preferred_element_...  15.8 us
    reduce_sum x2, other arithmetic, depthwise(): padded[:, vertical:vertical + SIDE, across:across + SIDE, :]  14.9 us
  transfers between devices with their start and end apart: 4, of which 3 were waited for; matrix products, arithmetic and copies ran while one was open for 22% of the time, Pallas kernels for 0%

commit v1 on v0

v1 whole, which is shorter than its diff:
```python
import math
from functools import partial

import jax
import jax.numpy as jnp
from jax import lax
from jax.experimental import pallas as pl
from jax.experimental.pallas import tpu as pltpu
from jax.sharding import PartitionSpec as P

KERNEL = 7
SIDE = 7
MARGIN = KERNEL // 2
POSITIONS = SIDE * SIDE
LANES = 128
EPSILON = 1e-06
VMEM_LIMIT = 56 * 1024 * 1024
AXES = ("enc", "slide")


def layer_norm(values, gain, shift):
    center = values - jnp.mean(values, axis=-1, keepdims=True)
    spread = jnp.mean(center * center, axis=-1, keepdims=True)
    return center * lax.rsqrt(spread + EPSILON) * gain + shift


def whole_vmem(count):
    return [pl.BlockSpec(memory_space=pltpu.VMEM)] * count


def prepare_kernel(x_ref, k_ref, bias_ref, gain_ref, shift_ref, normed_ref, hat_ref, rstd_ref, fsum_ref, xs, ks):
    tiles, channels = x_ref.shape[1], x_ref.shape[2]
    ks[...] = k_ref[...].astype(jnp.float32)

    def block(c, carry):
        lanes = pl.ds(pl.multiple_of(c * LANES, LANES), LANES)
        total = jnp.zeros((tiles, LANES), jnp.float32)
        for p in range(POSITIONS):
            value = x_ref[p, :, lanes].astype(jnp.float32)
            xs[p] = value
            total = total + value
        fsum_ref[:, lanes] = total
        bias = jnp.broadcast_to(bias_ref[:, lanes].astype(jnp.float32), (tiles, LANES))
        for i in range(SIDE):
            accs = [bias for _ in range(SIDE)]
            for a in range(KERNEL):
                row = i + a - MARGIN
                if row < 0 or row >= SIDE:
                    continue
                weights = [ks[pl.ds(a * KERNEL + b, 1), lanes] for b in range(KERNEL)]
                for col in range(SIDE):
                    value = xs[row * SIDE + col]
                    for j in range(SIDE):
                        b = col - j + MARGIN
                        if 0 <= b < KERNEL:
                            accs[j] = accs[j] + value * weights[b]
            for j in range(SIDE):
                rows = pl.ds((i * SIDE + j) * tiles, tiles)
                hat_ref[rows, lanes] = accs[j]
        return carry

    lax.fori_loop(0, channels // LANES, block, 0)
    gain = gain_ref[...].astype(jnp.float32)
    shift = shift_ref[...].astype(jnp.float32)

    def norm(p, carry):
        rows = pl.ds(pl.multiple_of(p * tiles, tiles), tiles)
        conv = hat_ref[rows, :]
        center = conv - jnp.mean(conv, axis=-1, keepdims=True)
        spread = jnp.mean(center * center, axis=-1, keepdims=True)
        rstd = lax.rsqrt(spread + EPSILON)
        hat = center * rstd
        hat_ref[rows, :] = hat
        normed_ref[rows, :] = (hat * gain + shift).astype(jnp.bfloat16)
        rstd_ref[rows, :] = jnp.broadcast_to(rstd, (tiles, LANES))
        return carry

    lax.fori_loop(0, POSITIONS, norm, 0, unroll=7)


def prepare(x, kernel, bias, gain, shift):
    positions, tiles, channels = x.shape
    rows = positions * tiles
    return pl.pallas_call(
        prepare_kernel,
        out_shape=(
            jax.ShapeDtypeStruct((rows, channels), jnp.bfloat16),
            jax.ShapeDtypeStruct((rows, channels), jnp.float32),
            jax.ShapeDtypeStruct((rows, LANES), jnp.float32),
            jax.ShapeDtypeStruct((tiles, channels), jnp.float32),
        ),
        in_specs=whole_vmem(5),
        out_specs=tuple(whole_vmem(4)),
        scratch_shapes=[
            pltpu.VMEM((positions, tiles, LANES), jnp.float32),
            pltpu.VMEM((positions, channels), jnp.float32),
        ],
        compiler_params=pltpu.CompilerParams(vmem_limit_bytes=VMEM_LIMIT),
        cost_estimate=pl.CostEstimate(flops=40_000_000, bytes_accessed=5_000_000, transcendentals=0),
    )(x, kernel, bias, gain, shift)


ROWS_STEP = 112


def hidden_kernel(normed_ref, w_ref, bias_ref, pooled_ref, slope_ref, hid):
    rows = normed_ref.shape[0]
    tiles, width = pooled_ref.shape
    hid[...] = lax.dot_general(
        normed_ref[...], w_ref[...], (((1,), (1,)), ((), ())), preferred_element_type=jnp.float32
    )
    bias = bias_ref[...].astype(jnp.float32)
    for c in range(width // LANES):
        lanes = slice(c * LANES, (c + 1) * LANES)
        part_bias = jnp.broadcast_to(bias[:, lanes], (tiles, LANES))

        def step(p, total):
            at = pl.ds(pl.multiple_of(p * tiles, tiles), tiles)
            h = hid[at, lanes] + part_bias
            cdf = 0.5 + 0.5 * lax.erf(h * (0.5 ** 0.5))
            pdf = jnp.exp(h * h * -0.5) * ((2.0 * math.pi) ** -0.5)
            active = (h * cdf).astype(jnp.bfloat16)
            slope_ref[at, lanes] = cdf + h * pdf
            return total + active.astype(jnp.float32)

        pooled_ref[:, lanes] = lax.fori_loop(
            0, rows // tiles, step, jnp.zeros((tiles, LANES), jnp.float32), unroll=7
        )


def hidden_layer(normed, w_in, in_bias, tiles):
    rows, channels = normed.shape
    ff = w_in.shape[0]
    width = 512
    return pl.pallas_call(
        hidden_kernel,
        grid=(ff // width,),
        out_shape=(
            jax.ShapeDtypeStruct((tiles, ff), jnp.float32),
            jax.ShapeDtypeStruct((rows, ff), jnp.float32),
        ),
        in_specs=[
            pl.BlockSpec((rows, channels), lambda f: (0, 0)),
            pl.BlockSpec((width, channels), lambda f: (f, 0)),
            pl.BlockSpec((1, width), lambda f: (0, f)),
        ],
        out_specs=(
            pl.BlockSpec((tiles, width), lambda f: (0, f)),
            pl.BlockSpec((rows, width), lambda f: (0, f)),
        ),
        scratch_shapes=[pltpu.VMEM((rows, width), jnp.float32)],
        compiler_params=pltpu.CompilerParams(vmem_limit_bytes=VMEM_LIMIT),
        cost_estimate=pl.CostEstimate(
            flops=2 * rows * ff * channels, bytes_accessed=20_000_000, transcendentals=rows * ff
        ),
    )(normed, w_in, in_bias)


def grad_hidden_kernel(slope_ref, ga_ref, normed_ref, gh_ref, gw_ref, gb_ref):
    rows = slope_ref.shape[0]
    tiles, width = ga_ref.shape
    for c in range(width // LANES):
        lanes = slice(c * LANES, (c + 1) * LANES)
        grad = ga_ref[:, lanes]

        def step(p, total):
            at = pl.ds(pl.multiple_of(p * tiles, tiles), tiles)
            wide = slope_ref[at, lanes] * grad
            gh_ref[at, lanes] = wide.astype(jnp.bfloat16)
            return total + wide

        total = lax.fori_loop(
            0, rows // tiles, step, jnp.zeros((tiles, LANES), jnp.float32), unroll=7
        )
        gb_ref[:, lanes] = jnp.sum(total, axis=0, keepdims=True)
    gw_ref[...] = lax.dot_general(
        gh_ref[...], normed_ref[...], (((0,), (0,)), ((), ())), preferred_element_type=jnp.float32
    )


def grad_hidden_layer(slope, grad_active, normed):
    rows, ff = slope.shape
    tiles = grad_active.shape[0]
    channels = normed.shape[1]
    width = 512
    return pl.pallas_call(
        grad_hidden_kernel,
        grid=(ff // width,),
        out_shape=(
            jax.ShapeDtypeStruct((rows, ff), jnp.bfloat16),
            jax.ShapeDtypeStruct((ff, channels), jnp.float32),
            jax.ShapeDtypeStruct((1, ff), jnp.float32),
        ),
        in_specs=[
            pl.BlockSpec((rows, width), lambda f: (0, f)),
            pl.BlockSpec((tiles, width), lambda f: (0, f)),
            pl.BlockSpec((rows, channels), lambda f: (0, 0)),
        ],
        out_specs=(
            pl.BlockSpec((rows, width), lambda f: (0, f)),
            pl.BlockSpec((width, channels), lambda f: (f, 0)),
            pl.BlockSpec((1, width), lambda f: (0, f)),
        ),
        compiler_params=pltpu.CompilerParams(vmem_limit_bytes=VMEM_LIMIT),
        cost_estimate=pl.CostEstimate(
            flops=2 * rows * ff * channels, bytes_accessed=25_000_000, transcendentals=0
        ),
    )(slope, grad_active, normed)


def prepare_back_kernel(gn_ref, hat_ref, rstd_ref, x_ref, gain_ref, out_ref, gc, xs):
    tiles, channels = x_ref.shape[1], x_ref.shape[2]
    gain = gain_ref[...].astype(jnp.float32)

    def norm(p, carry):
        total_gain, total_shift = carry
        rows = pl.ds(pl.multiple_of(p * tiles, tiles), tiles)
        grad = gn_ref[rows, :]
        hat = hat_ref[rows, :]
        rstd = rstd_ref[rows, 0:1]
        scaled = grad * gain
        first = jnp.mean(scaled, axis=-1, keepdims=True)
        second = jnp.mean(scaled * hat, axis=-1, keepdims=True)
        gc[p] = rstd * (scaled - first - hat * second)
        return (total_gain + grad * hat, total_shift + grad)

    zero = jnp.zeros((tiles, channels), jnp.float32)
    total_gain, total_shift = lax.fori_loop(0, POSITIONS, norm, (zero, zero))
    out_ref[pl.ds(POSITIONS + 1, 1), :] = jnp.sum(total_gain, axis=0, keepdims=True)
    out_ref[pl.ds(POSITIONS + 2, 1), :] = jnp.sum(total_shift, axis=0, keepdims=True)

    def block(c, carry):
        lanes = pl.ds(pl.multiple_of(c * LANES, LANES), LANES)
        total = jnp.zeros((tiles, LANES), jnp.float32)
        for p in range(POSITIONS):
            xs[p] = x_ref[p, :, lanes].astype(jnp.float32)
            total = total + gc[p, :, lanes]
        out_ref[pl.ds(POSITIONS, 1), lanes] = jnp.sum(total, axis=0, keepdims=True)
        for a in range(KERNEL):
            accs = [jnp.zeros((tiles, LANES), jnp.float32) for _ in range(KERNEL)]
            for i in range(SIDE):
                row = i + a - MARGIN
                if row < 0 or row >= SIDE:
                    continue
                grads = [gc[i * SIDE + j, :, lanes] for j in range(SIDE)]
                for col in range(SIDE):
                    value = xs[row * SIDE + col]
                    for j in range(SIDE):
                        b = col - j + MARGIN
                        if 0 <= b < KERNEL:
                            accs[b] = accs[b] + value * grads[j]
            for b in range(KERNEL):
                out_ref[pl.ds(a * KERNEL + b, 1), lanes] = jnp.sum(accs[b], axis=0, keepdims=True)
        return carry

    lax.fori_loop(0, channels // LANES, block, 0)


def prepare_back(grad_normed, hat, rstd, x, gain):
    positions, tiles, channels = x.shape
    return pl.pallas_call(
        prepare_back_kernel,
        out_shape=jax.ShapeDtypeStruct((positions + 3, channels), jnp.float32),
        in_specs=whole_vmem(5),
        out_specs=pl.BlockSpec(memory_space=pltpu.VMEM),
        scratch_shapes=[
            pltpu.VMEM((positions, tiles, channels), jnp.float32),
            pltpu.VMEM((positions, tiles, LANES), jnp.float32),
        ],
        compiler_params=pltpu.CompilerParams(vmem_limit_bytes=VMEM_LIMIT),
        cost_estimate=pl.CostEstimate(flops=40_000_000, bytes_accessed=8_000_000, transcendentals=0),
    )(grad_normed, hat, rstd, x, gain)


def swap(values, bit, devices):
    pairs = [(d, d ^ (1 << bit)) for d in range(devices)]
    return lax.ppermute(values, AXES, pairs)


def halve_scatter(partial_sum, order, narrow, devices, index):
    bits = devices.bit_length() - 1
    rows, columns = partial_sum.shape
    current = partial_sum.reshape((2,) * bits + (rows // devices, columns))
    left = list(range(bits - 1, -1, -1))
    for bit in order:
        axis = left.index(bit)
        left.pop(axis)
        mine = (index >> bit) & 1
        kept = lax.dynamic_index_in_dim(current, mine, axis, keepdims=False)
        sent = lax.dynamic_index_in_dim(current, 1 - mine, axis, keepdims=False)
        if bit in narrow:
            sent = sent.astype(jnp.bfloat16)
        shape = sent.shape
        flat = sent.reshape(-1, columns)
        current = kept + swap(flat, bit, devices).reshape(shape).astype(jnp.float32)
    return current


def per_device(
    tile_features, tile_slide, slide_order, targets, dw_kernel, dw_bias, norm_gain, norm_bias,
    w_in, in_bias, w_out, out_bias, layer_scale, final_gain, final_bias, head_weight, head_bias,
):
    highest = lax.Precision.HIGHEST
    f32 = jnp.float32
    bf16 = jnp.bfloat16
    tiles, channels = tile_features.shape[0], tile_features.shape[-1]
    ff = w_in.shape[0]
    n_enc, n_slide = lax.axis_size("enc"), lax.axis_size("slide")
    devices = n_enc * n_slide
    slides = slide_order.shape[1]
    owned = slides // n_slide
    genes = targets.shape[-1]
    enc_index, slide_index = lax.axis_index("enc"), lax.axis_index("slide")
    index = enc_index * n_slide + slide_index

    hot = (tile_slide == slide_order).astype(f32)
    tally = jnp.pad(jnp.sum(hot, axis=0)[None, :], ((0, 0), (0, -slides % genes)))
    early = lax.all_gather(
        jnp.concatenate([targets[0], tally.reshape(-1, genes)], axis=0), "slide"
    )
    all_targets = early[:, :owned].reshape(slides, genes)
    counts = jnp.sum(early[:, owned:].reshape(n_slide, -1), axis=0)[:slides]
    divisor = jnp.maximum(counts, 1.0)[:, None]

    x = jnp.transpose(tile_features, (1, 2, 0, 3)).reshape(POSITIONS, tiles, channels)
    normed, hat, rstd, feature_sum = prepare(
        x, dw_kernel, dw_bias[None, :], norm_gain[None, :], norm_bias[None, :]
    )
    pooled_active, slope = hidden_layer(normed, w_in, in_bias[None, :], tiles)
    high = lax.reduce_precision(pooled_active, 8, 7)
    both = jnp.concatenate([high, pooled_active - high], axis=0).astype(bf16)
    product = jnp.dot(both, w_out, preferred_element_type=f32)
    branch = (product[:tiles] + product[tiles:]) / POSITIONS + out_bias.astype(f32)
    scale = layer_scale.astype(f32)
    pooled = feature_sum / POSITIONS + scale * branch
    embedded, pull_norm = jax.vjp(
        layer_norm, pooled, final_gain.astype(f32), final_bias.astype(f32)
    )
    partial_sums = lax.dot_general(
        hot.astype(bf16), embedded.astype(bf16), (((0,), (0,)), ((), ())),
        preferred_element_type=f32,
    )
    slide_mean = jnp.sum(lax.all_gather(partial_sums, "slide"), axis=0) / divisor
    head_wide = head_weight.astype(f32)
    prediction = jnp.dot(
        slide_mean, head_wide, precision=highest, preferred_element_type=f32
    ) + head_bias.astype(f32)
    difference = prediction - all_targets
    losses = 0.5 * jnp.mean(difference * difference, axis=-1)
    slide_loss = lax.dynamic_slice_in_dim(losses, slide_index * owned, owned)
    grad_pred = difference / genes
    grad_mean = lax.dot_general(
        grad_pred, head_wide, (((1,), (1,)), ((), ())), precision=highest,
        preferred_element_type=f32,
    )
    slide_grad = (grad_mean / divisor).astype(bf16)
    grad_embed = jnp.dot(hot.astype(bf16), slide_grad, preferred_element_type=f32)
    grad_pooled, grad_fgain, grad_fbias = pull_norm(grad_embed)
    grad_scale = jnp.sum(grad_pooled * branch, axis=0)
    scaled = grad_pooled * scale
    grad_out_bias = jnp.sum(scaled, axis=0)
    grad_projected = (scaled / POSITIONS).astype(bf16)
    grad_active = lax.dot_general(
        grad_projected, w_out, (((1,), (1,)), ((), ())), preferred_element_type=f32
    )
    grad_hidden, partial_w_in, grad_inner = grad_hidden_layer(slope, grad_active, normed)

    bits = devices.bit_length() - 1
    inner = n_slide.bit_length() - 1
    xs = list(range(1, inner))
    rest = list(range(inner, bits))
    half = channels // 2
    narrow = (1, inner)
    first = halve_scatter(
        partial_w_in[:, :half], [0] + xs + rest, narrow, devices, index
    )
    second = halve_scatter(
        partial_w_in[:, half:], [0] + rest[:1] + xs + rest[1:], narrow, devices, index
    )
    grad_w_in = jnp.concatenate([first, second], axis=1)

    grad_normed = jnp.dot(grad_hidden, w_in, preferred_element_type=f32)
    small = prepare_back(grad_normed, hat, rstd, x, norm_gain[None, :])
    bundle = jnp.concatenate(
        [
            small, grad_out_bias[None], grad_scale[None], grad_fgain[None], grad_fbias[None],
            grad_inner.reshape(-1, channels),
        ],
        axis=0,
    )
    used = bundle.shape[0]
    bundle = jnp.pad(bundle, ((0, -used % 64), (0, 0)))
    lines = bundle.reshape(devices, -1)
    lines = lax.all_to_all(lines, AXES, split_axis=0, concat_axis=0, tiled=True)
    bundle = lax.all_gather(jnp.sum(lines, axis=0), AXES).reshape(-1, channels)

    head_parts = lax.all_gather(
        jnp.concatenate([slide_mean, grad_pred], axis=1), "enc"
    ).reshape(n_enc * slides, channels + genes)
    grad_head_w = lax.dot_general(
        head_parts[:, :channels], head_parts[:, channels:], (((0,), (0,)), ((), ())),
        precision=highest, preferred_element_type=f32,
    )
    grad_head_b = jnp.sum(head_parts[:, channels:], axis=0)

    mine = pooled_active.reshape(tiles, devices, ff // devices).transpose(1, 0, 2)
    mine = lax.all_to_all(mine, AXES, split_axis=0, concat_axis=0, tiled=True)
    mine = mine.reshape(devices * tiles, ff // devices)
    mine_high = lax.reduce_precision(mine, 8, 7)
    all_grad = lax.all_gather(grad_projected, AXES, tiled=True)

    def rows_product(left):
        return lax.dot_general(
            left.astype(bf16), all_grad, (((0,), (0,)), ((), ())), preferred_element_type=f32
        )

    grad_w_out = rows_product(mine_high) + rows_product(mine - mine_high)
    taps = POSITIONS
    return (
        grad_w_in,
        grad_w_out,
        bundle[:taps],
        bundle[taps : taps + 7],
        bundle[taps + 7 : used].reshape(-1),
        grad_head_w,
        grad_head_b,
        slide_loss[None, :],
    )


def solution(mesh):
    placed = (
        P(AXES, None, None, None),
        P(AXES, None),
        P("enc", None),
        P("enc", "slide", None),
    ) + (P(),) * 13
    return jax.shard_map(
        per_device,
        mesh=mesh,
        in_specs=placed,
        out_specs=(P(AXES, None), P(AXES, None), P(), P(), P(), P(), P(), P("enc", "slide")),
        check_vma=False,
    )
```

time: 510 us -> 303 us (0.59)
  waiting for transfers between devices: 253 us -> 42 us
  blocking collectives: 50 us -> 129 us
  Pallas kernels: 0 us -> 61.3 us
  matrix products: 76.4 us -> 18.8 us
  other arithmetic: 64.7 us -> 12.2 us
  local copies, waits for them, and re-layouts: 41.7 us -> 23.6 us
  between operations: 15 us -> 1.18 us
  starting transfers between devices: 8.43 us -> 14.5 us
    psum x1 -> x0, waiting for transfers between devices: 132 us -> none  [per_device(): lax.psum((grad_kernel, grad_vectors, grad_inner, grad_head_w, grad_head_b...]
    all_gather x0 -> x5, blocking collectives: none -> 129 us  [the longest x1 43 us: per_device(): all_grad = lax.all_gather(grad_projected, AXES, tiled=True)]
    unnamed x3 -> x0, waiting for transfers between devices: 118 us -> none
    pallas_call x0 -> x4, Pallas kernels: none -> 61.3 us  [the longest x1 17.6 us: prepare(): pl.pallas_call(prepare_kernel, out_shape=(jax.ShapeDtypeStruct((rows, cha...]
    dot_general x10 -> x9, matrix products: 75.9 us -> 18.4 us  [the longest x1 9.09 us: per_device(): grad_normed = jnp.dot(grad_hidden, w_in, preferred_element_type=f32)]
    psum x1 -> x0, blocking collectives: 43.6 us -> none  [per_device(): lax.psum((grad_kernel, grad_vectors, grad_inner, grad_head_w, grad_head_b...]
    ppermute x0 -> x10, waiting for transfers between devices: none -> 42 us  [swap(): return lax.ppermute(values, AXES, pairs)]
    reduce_sum x15 -> x6, other arithmetic: 34 us -> 2.67 us  [the longest x1 1.06 us: per_device(): bundle = lax.all_gather(jnp.sum(lines, axis=0), AXES).reshape(-1, channels)]
  transfers between devices with their start and end apart: 4 -> 12, of which waited for: 3 -> 8; matrix products, arithmetic and copies ran while one was open for 22% -> 8% of each run, Pallas kernels for 0% -> 5%
where the time goes in v1:
time: 303 us; the launch traced here: 302 us
  blocking collectives  129 us (43%)
  Pallas kernels  61.3 us (20%)
  waiting for transfers between devices  42 us (14%)
  local copies, waits for them, and re-layouts  23.6 us (8%)
  matrix products  18.8 us (6%)
  starting transfers between devices  14.5 us (5%)
  other arithmetic  12.2 us (4%)
    all_gather x1, blocking collectives, per_device(): all_grad = lax.all_gather(grad_projected, AXES, tiled=True)  43 us
    all_gather x1, blocking collectives, per_device(): bundle = lax.all_gather(jnp.sum(lines, axis=0), AXES).reshape(-1, channels)  42.2 us
    ppermute x10, waiting for transfers between devices, swap(): return lax.ppermute(values, AXES, pairs)  42 us
    all_gather x1, blocking collectives, per_device(): lax.all_gather(jnp.concatenate([slide_mean, grad_pred], axis=1), 'enc')  31.8 us
    pallas_call x1, Pallas kernels, prepare(): pl.pallas_call(prepare_kernel, out_shape=(jax.ShapeDtypeStruct((rows, cha...  17.6 us
    pallas_call x1, Pallas kernels, prepare_back(): pl.pallas_call(prepare_back_kernel, out_shape=jax.ShapeDtypeStruct((posit...  16 us
    pallas_call x1, Pallas kernels, hidden_layer(): pl.pallas_call(hidden_kernel, grid=(ff // width,), out_shape=(jax.ShapeDt...  14.1 us
    pallas_call x1, Pallas kernels, grad_hidden_layer(): pl.pallas_call(grad_hidden_kernel, grid=(ff // width,), out_shape=(jax.Sh...  13.5 us
  transfers between devices with their start and end apart: 12, of which 8 were waited for; matrix products, arithmetic and copies ran while one was open for 8% of the time, Pallas kernels for 5%

profile of v1, /device:TPU:0, one launch (start us, length us, event | category | flops | bytes accessed | tf_op | source)
XLA Modules:
  0.0 302.3 jit_solution(249155512915707523)
XLA Ops:
  0.6 0.9 convert_reduce_fusion
  1.6 0.7 fusion.18
  2.2 6.2 %all-gather.4 = f32[4,3,256]{2,1,0:T(4,128)S(1)} all-gather(f32[1,3,256]{2,1,0:T(4,128)S(1)} %fusion.18), channel_id=3, replica_groups=mesh['enc'=8,'slide'=4] {'slide'}, dimensions={0}, use_global_device_ids=true | all-gather | bytes 15360 | tf_op jit(solution)/shard_map/all_gather | solution.py:318
  8.4 1.3 broadcast_in_dim.21.gain_ref
  9.7 1.3 broadcast_in_dim.20.bias_ref
  11.0 1.3 broadcast_in_dim.44.shift_ref
  12.2 1.3 broadcast_in_dim.45.bias_ref
  13.5 17.6 %shard_map.224 = (bf16[784,768]{1,0:T(8,128)(2,1)}, f32[784,768]{1,0:T(8,128)}, f32[784,128]{1,0:T(8,128)}, f32[16,768]{1,0:T(8,128)}) custom-call(bf16[49,16,768]{2,1,0:T(8,128)(2,1)} %bitcast.86, bf16[49,768]{1,0:T(8,128)(2,1)} %k_ref.1, bf16[1,768]{1,0:T(2,128)(2,1)} %broadcast_in_dim.20.bias_ref, bf16[1,768]{1,0:T(2,128)(2,1)} %broadcast_in_dim.21.gain_ref, ...), custom_call_target="tpu_custom_call" | custom-call | flops 40000000 | bytes 5000000 | tf_op jit(solution)/shard_map/pallas_call | solution.py:84
  31.2 14.1 %shard_map.225 = (f32[16,3072]{1,0:T(8,128)}, f32[784,3072]{1,0:T(8,128)}) custom-call(bf16[784,768]{1,0:T(8,128)(2,1)} %get-tuple-element.17.normed_ref, bf16[3072,768]{1,0:T(8,128)(2,1)} %w_ref.1, bf16[1,3072]{1,0:T(2,128)(2,1)} %broadcast_in_dim.45.bias_ref), custom_call_target="tpu_custom_call" | custom-call | flops 3699376128 | bytes 20000000 | tf_op jit(solution)/shard_map/pallas_call | solution.py:135
  45.3 0.9 reduce-precision_convert_fusion.1
  46.4 0.9 fusion.6
  47.8 5.5 %all-gather = f32[32,768]{1,0:T(8,128)S(1)} all-gather(f32[8,768]{1,0:T(8,128)S(1)} %fusion.13), channel_id=2, replica_groups=mesh['enc'=8,'slide'=4] {'slide'}, dimensions={0}, use_global_device_ids=true | all-gather | bytes 122880 | tf_op jit(solution)/shard_map/all_gather | solution.py:343
  55.1 4.4 %fusion.29.ga_ref = f32[16,3072]{1,0:T(8,128)} fusion(bf16[16,768]{1,0:T(8,128)(2,1)S(1)} %get-tuple-element.41, bf16[3072,768]{1,0:T(8,128)(2,1)} %param.27), kind=kOutput, calls=%fused_computation.86 | convolution fusion | flops 75497472 | bytes 4939776 | tf_op jit(solution)/shard_map/dot_general | solution.py:363
  59.4 13.5 %shard_map.226 = (bf16[784,3072]{1,0:T(8,128)(2,1)}, f32[3072,768]{1,0:T(8,128)}, f32[1,3072]{1,0:T(1,128)}) custom-call(f32[784,3072]{1,0:T(8,128)} %get-tuple-element.18.slope_ref, f32[16,3072]{1,0:T(8,128)} %fusion.29.ga_ref, bf16[784,768]{1,0:T(8,128)(2,1)} %get-tuple-element.17.normed_ref), custom_call_target="tpu_custom_call" | custom-call | flops 3699376128 | bytes 25000000 | tf_op jit(solution)/shard_map/pallas_call | solution.py:186
  73.0 8.0 %fusion.28 = (f32[3072,384]{1,0:T(8,128)}, f32[3072,384]{1,0:T(8,128)}) fusion(f32[3072,768]{1,0:T(8,128)} %get-tuple-element.21), kind=kLoop, calls=%fused_computation.85 | loop fusion | bytes 18874368 | tf_op jit(solution)/shard_map/slice | solution.py:375
  81.0 2.0 constant_dynamic-slice_fusion.3
  83.4 0.6 copy-done.2
  84.0 1.6 constant_dynamic-slice_fusion.1
  86.5 0.7 reduce.5
  87.2 9.1 %fusion.31.gn_ref = f32[784,768]{1,0:T(8,128)} fusion(bf16[784,3072]{1,0:T(8,128)(2,1)} %get-tuple-element.22, bf16[3072,768]{1,0:T(8,128)(2,1)} %w_ref.1), kind=kOutput, calls=%fused_computation.88 | convolution fusion | flops 3699376128 | bytes 11943936 | tf_op jit(solution)/shard_map/dot_general | solution.py:382
  96.3 16.0 %shard_map.227 = f32[52,768]{1,0:T(8,128)} custom-call(f32[784,768]{1,0:T(8,128)} %fusion.31.gn_ref, f32[784,768]{1,0:T(8,128)} %get-tuple-element.23.hat_ref, f32[784,128]{1,0:T(8,128)} %get-tuple-element.24.rstd_ref, bf16[49,16,768]{2,1,0:T(8,128)(2,1)} %bitcast.87, bf16[1,768]{1,0:T(2,128)(2,1)} %broadcast_in_dim.21.gain_ref), custom_call_target="tpu_custom_call" | custom-call | flops 40000000 | bytes 8000000 | tf_op jit(solution)/shard_map/pallas_call | solution.py:261
  112.4 1.0 concatenate.19
  113.4 0.9 all_to_all.12
  114.2 6.2 %all-to-all-start.1 = ((f32[32,1,1536]{2,1,0:T(1,128)}), f32[32,1,1536]{2,1,0:T(1,128)}, u32[]{:S(2)}, u32[]{:S(2)}) async-start(f32[32,1,1536]{2,1,0:T(1,128)} %all_to_all.12), calls=%async_computation.1 | async-start | bytes 393216 | tf_op jit(solution)/shard_map/all_to_all | solution.py:394
  120.6 0.9 copy.36
  121.5 31.8 %all-gather.3 = f32[64,1024]{1,0:T(8,128)S(1)} all-gather(f32[8,1024]{1,0:T(8,128)S(1)} %pad_maximum_fusion.1), channel_id=5, replica_groups=mesh['enc'=8,'slide'=4] {'enc'}, dimensions={0}, use_global_device_ids=true | all-gather | bytes 294912 | tf_op jit(solution)/shard_map/all_gather | solution.py:397
  153.3 0.6 slice_reduce_fusion
  153.9 43.0 %all_gather.31 = bf16[512,768]{1,0:T(8,128)(2,1)S(1)} all-gather(bf16[16,768]{1,0:T(8,128)(2,1)} %copy-done.4), channel_id=1, replica_groups=mesh['enc'=8,'slide'=4] {'enc','slide'}, dimensions={0}, use_global_device_ids=true | all-gather | bytes 811008 | tf_op jit(solution)/shard_map/all_gather | solution.py:410
  196.9 3.5 %all-to-all-start = ((f32[32,16,96]{2,1,0:T(8,128)}), f32[32,16,96]{2,1,0:T(8,128)}, u32[]{:S(2)}, u32[]{:S(2)}) async-start(f32[32,16,96]{2,1,0:T(8,128)} %bitcast.89), calls=%async_computation | async-start | bytes 524288 | tf_op jit(solution)/shard_map/all_to_all | solution.py:407
  200.4 0.6 dynamic-slice_bitcast_fusion.2
  201.0 1.7 fusion.4
  202.7 1.1 reduce_sum.153
  203.7 42.2 %all-gather.5 = f32[32,1,1536]{2,1,0:T(1,128)S(1)} all-gather(f32[1,1,1536]{2,1,0:T(1,128)S(1)} %reshape.181), channel_id=4, replica_groups=mesh['enc'=8,'slide'=4] {'enc','slide'}, dimensions={0}, use_global_device_ids=true | all-gather | bytes 202752 | tf_op jit(solution)/shard_map/all_gather | solution.py:395
  246.0 0.6 slice.60
  246.6 0.7 reshape.174
  247.3 0.6 reshape.175
  247.9 1.0 fusion.2
  248.9 4.4 %bitcast_add_fusion = (f32[2,2,2,2,96,384]{5,4,3,2,1,0:T(8,128)S(1)}, f32[2,2,2,2,96,384]{5,4,3,2,1,0:T(8,128)S(1)}) fusion(f32[2,2,2,2,96,384]{5,4,3,2,1,0:T(8,128)} %bitcast.26, f32[2,2,2,2,2,96,384]{6,5,4,3,2,1,0:T(8,128)} %bitcast.84, s32[]{:T(128)S(6)} %select_n.49, f32[2,2,2,2,96,384]{5,4,3,2,1,0:T(8,128)} %bitcast.11, ...), kind=kLoop, calls=%fused_computation | loop fusion | flops 1179648 | bytes 14155780 | tf_op jit(solution)/shard_map/add | solution.py:295
  253.9 1.0 convolution_add_fusion
  254.9 14.1 %collective-permute-done.1 = bf16[768,384]{1,0:T(8,128)(2,1)S(1)} collective-permute-done((bf16[768,384]{1,0:T(8,128)(2,1)S(1)}, bf16[768,384]{1,0:T(8,128)(2,1)S(1)}, u32[]{:S(2)}, u32[]{:S(2)}) %collective-permute-start.1) | collective-permute-done | bytes 589856 | tf_op jit(solution)/shard_map/ppermute | solution.py:277
  269.7 1.8 collective-permute-start.7
  271.5 6.3 %collective-permute-done.2 = bf16[384,384]{1,0:T(8,128)(2,1)S(1)} collective-permute-done((bf16[384,384]{1,0:T(8,128)(2,1)S(1)}, bf16[384,384]{1,0:T(8,128)(2,1)S(1)}, u32[]{:S(2)}, u32[]{:S(2)}) %collective-permute-start.2) | collective-permute-done | bytes 294944 | tf_op jit(solution)/shard_map/ppermute | solution.py:277
  278.3 1.8 collective-permute-start.8
  280.1 8.6 %collective-permute-done.3 = f32[192,384]{1,0:T(8,128)S(1)} collective-permute-done((f32[192,384]{1,0:T(8,128)S(1)}, f32[192,384]{1,0:T(8,128)S(1)}, u32[]{:S(2)}, u32[]{:S(2)}) %collective-permute-start.3) | collective-permute-done | bytes 294944 | tf_op jit(solution)/shard_map/ppermute | solution.py:277
  288.8 4.5 %collective-permute-done.8 = f32[192,384]{1,0:T(8,128)S(1)} collective-permute-done((f32[192,384]{1,0:T(8,128)S(1)}, f32[192,384]{1,0:T(8,128)S(1)}, u32[]{:S(2)}, u32[]{:S(2)}) %collective-permute-start.8) | collective-permute-done | bytes 294944 | tf_op jit(solution)/shard_map/ppermute | solution.py:277
  293.5 6.4 %collective-permute-done.4 = f32[96,384]{1,0:T(8,128)S(1)} collective-permute-done((f32[96,384]{1,0:T(8,128)S(1)}, f32[96,384]{1,0:T(8,128)S(1)}, u32[]{:S(2)}, u32[]{:S(2)}) %collective-permute-start.4) | collective-permute-done | bytes 147488 | tf_op jit(solution)/shard_map/ppermute | solution.py:277
  299.9 1.7 collective-permute-done.9
  301.6 0.7 pad_maximum_fusion
  (102 shorter events, 5.8 us)
Async XLA Ops:
  0.6 52.8 %copy-start = (bf16[768,256]{1,0:T(8,128)(2,1)S(1)}, bf16[768,256]{1,0:T(8,128)(2,1)}, u32[]{:S(2)}) copy-start(bf16[768,256]{1,0:T(8,128)(2,1)} %param.32) | copy-start | bytes 1179652
  8.4 36.8 %copy-start.5 = (f32[4,3,256]{2,1,0:T(4,128)}, f32[4,3,256]{2,1,0:T(4,128)S(1)}, u32[]{:S(2)}) copy-start(f32[4,3,256]{2,1,0:T(4,128)S(1)} %all-gather.4) | copy-start | bytes 36868
  13.5 32.7 %slice-start = ((s8[4718592]{0:T(1024)(128)(4,1)}), s8[4194304]{0:T(1024)(128)(4,1)S(1)}, s32[]{:S(2)}) async-start(s8[4718592]{0:T(1024)(128)(4,1)} %bitcast.80), calls=%async_computation.2 | async-start | bytes 8388608
  31.2 15.0 %copy-start.8 = (bf16[768]{0:T(1024)(128)(2,1)S(1)}, bf16[768]{0:T(1024)(128)(2,1)}, u32[]{:S(2)}) copy-start(bf16[768]{0:T(1024)(128)(2,1)} %param.29) | copy-start | bytes 4612
  31.2 15.1 %copy-start.9 = (bf16[768]{0:T(1024)(128)(2,1)S(1)}, bf16[768]{0:T(1024)(128)(2,1)}, u32[]{:S(2)}) copy-start(bf16[768]{0:T(1024)(128)(2,1)} %param.28) | copy-start | bytes 4612
  31.2 15.1 %slice-start.1 = ((s8[4718592]{0:T(1024)(128)(4,1)}), s8[524288]{0:T(1024)(128)(4,1)S(1)}, s32[]{:S(2)}) async-start(s8[4718592]{0:T(1024)(128)(4,1)} %bitcast.80), calls=%async_computation.3 | async-start | bytes 1048576
  46.3 0.9 copy-start.6
  46.3 1.3 copy-start.10
  46.3 1.3 copy-start.11
  46.3 1.3 copy-start.13
  46.3 1.3 copy-start.14
  46.3 7.0 %slice-start.2 = ((f32[4,3,256]{2,1,0:T(4,128)}), f32[4,2,256]{2,1,0:T(2,128)S(1)}, s32[]{:S(2)}) async-start(f32[4,3,256]{2,1,0:T(4,128)} %copy-done.5), calls=%async_computation.4 | async-start | bytes 16384 | tf_op jit(solution)/shard_map/slice | solution.py:321
  46.4 7.0 %copy-start.12 = (bf16[256]{0:T(256)(128)(2,1)S(1)}, bf16[256]{0:T(256)(128)(2,1)}, u32[]{:S(2)}) copy-start(bf16[256]{0:T(256)(128)(2,1)} %param.33) | copy-start | bytes 1540
  55.1 4.4 %copy-start.4 = (bf16[16,768]{1,0:T(8,128)(2,1)}, bf16[16,768]{1,0:T(8,128)(2,1)S(1)}, u32[]{:S(2)}) copy-start(bf16[16,768]{1,0:T(8,128)(2,1)S(1)} %get-tuple-element.41) | copy-start | bytes 73732
  81.0 3.0 %copy-start.2 = (f32[3072,384]{1,0:T(8,128)S(1)}, f32[3072,384]{1,0:T(8,128)}, u32[]{:S(2)}) copy-start(f32[3072,384]{1,0:T(8,128)} %get-tuple-element.36) | copy-start | bytes 14155780
  83.0 165.9 %collective-permute-start = (f32[1536,384]{1,0:T(8,128)S(1)}, f32[1536,384]{1,0:T(8,128)}, u32[]{:S(2)}, u32[]{:S(2)}) collective-permute-start(f32[1536,384]{1,0:T(8,128)S(1)} %bitcast.88), channel_id=1, source_target_pairs={{0,1},{1,0},{2,3},{3,2},{4,5},{5,4},{6,7},{7,6},{8,9},{9,8},{10,11... | collective-permute-start | bytes 7077896 | tf_op jit(solution)/shard_map/ppermute | solution.py:277
  84.0 2.5 copy-start.7
  85.6 163.3 %collective-permute-start.5 = (f32[1536,384]{1,0:T(8,128)}, f32[1536,384]{1,0:T(8,128)}, u32[]{:S(2)}, u32[]{:S(2)}) collective-permute-start(f32[1536,384]{1,0:T(8,128)} %bitcast.25), channel_id=1, source_target_pairs={{0,1},{1,0},{2,3},{3,2},{4,5},{5,4},{6,7},{7,6},{8,9},{9,8},{10,11... | collective-permute-start | bytes 7077896 | tf_op jit(solution)/shard_map/ppermute | solution.py:277
  96.3 24.1 %copy-start.3 = (f32[16,3072]{1,0:T(8,128)S(1)}, f32[16,3072]{1,0:T(8,128)}, u32[]{:S(2)}) copy-start(f32[16,3072]{1,0:T(8,128)} %get-tuple-element.20) | copy-start | bytes 589828
  114.2 82.6 %all-to-all-start.1 = ((f32[32,1,1536]{2,1,0:T(1,128)}), f32[32,1,1536]{2,1,0:T(1,128)}, u32[]{:S(2)}, u32[]{:S(2)}) async-start(f32[32,1,1536]{2,1,0:T(1,128)} %all_to_all.12), calls=%async_computation.1 | async-start | bytes 393216 | tf_op jit(solution)/shard_map/all_to_all | solution.py:394
  196.9 51.0 %all-to-all-start = ((f32[32,16,96]{2,1,0:T(8,128)}), f32[32,16,96]{2,1,0:T(8,128)}, u32[]{:S(2)}, u32[]{:S(2)}) async-start(f32[32,16,96]{2,1,0:T(8,128)} %bitcast.89), calls=%async_computation | async-start | bytes 524288 | tf_op jit(solution)/shard_map/all_to_all | solution.py:407
  253.4 15.6 %collective-permute-start.1 = (bf16[768,384]{1,0:T(8,128)(2,1)S(1)}, bf16[768,384]{1,0:T(8,128)(2,1)S(1)}, u32[]{:S(2)}, u32[]{:S(2)}) collective-permute-start(bf16[768,384]{1,0:T(8,128)(2,1)S(1)} %bitcast.93), channel_id=1, source_target_pairs={{0,2},{1,3},{2,0},{3,1},{4,6},{5,7},{6,4},{7,5},{8,10},{9,11},{10,... | collective-permute-start | bytes 1769480 | tf_op jit(solution)/shard_map/ppermute | solution.py:277
  253.8 15.6 %collective-permute-start.6 = (bf16[768,384]{1,0:T(8,128)(2,1)S(1)}, bf16[768,384]{1,0:T(8,128)(2,1)S(1)}, u32[]{:S(2)}, u32[]{:S(2)}) collective-permute-start(bf16[768,384]{1,0:T(8,128)(2,1)S(1)} %bitcast.92), channel_id=1, source_target_pairs={{0,4},{1,5},{2,6},{3,7},{4,0},{5,1},{6,2},{7,3},{8,12},{9,13},{10,... | collective-permute-start | bytes 1769480 | tf_op jit(solution)/shard_map/ppermute | solution.py:277
  269.2 8.5 %collective-permute-start.2 = (bf16[384,384]{1,0:T(8,128)(2,1)S(1)}, bf16[384,384]{1,0:T(8,128)(2,1)S(1)}, u32[]{:S(2)}, u32[]{:S(2)}) collective-permute-start(bf16[384,384]{1,0:T(8,128)(2,1)S(1)} %bitcast.98), channel_id=1, source_target_pairs={{0,4},{1,5},{2,6},{3,7},{4,0},{5,1},{6,2},{7,3},{8,12},{9,13},{10,... | collective-permute-start | bytes 884744 | tf_op jit(solution)/shard_map/ppermute | solution.py:277
  269.7 8.5 %collective-permute-start.7 = (bf16[384,384]{1,0:T(8,128)(2,1)S(1)}, bf16[384,384]{1,0:T(8,128)(2,1)S(1)}, u32[]{:S(2)}, u32[]{:S(2)}) collective-permute-start(bf16[384,384]{1,0:T(8,128)(2,1)S(1)} %bitcast.99), channel_id=1, source_target_pairs={{0,2},{1,3},{2,0},{3,1},{4,6},{5,7},{6,4},{7,5},{8,10},{9,11},{10,... | collective-permute-start | bytes 884744 | tf_op jit(solution)/shard_map/ppermute | solution.py:277
  277.8 10.8 %collective-permute-start.3 = (f32[192,384]{1,0:T(8,128)S(1)}, f32[192,384]{1,0:T(8,128)S(1)}, u32[]{:S(2)}, u32[]{:S(2)}) collective-permute-start(f32[192,384]{1,0:T(8,128)S(1)} %bitcast.100), channel_id=1, source_target_pairs={{0,8},{1,9},{2,10},{3,11},{4,12},{5,13},{6,14},{7,15},{8,0},{9,1},... | collective-permute-start | bytes 884744 | tf_op jit(solution)/shard_map/ppermute | solution.py:277
  278.2 24.1 %copy-start.1 = (bf16[768,256]{1,0:T(8,128)(2,1)S(1)}, bf16[768,256]{1,0:T(8,128)(2,1)}, u32[]{:S(2)}) copy-start(bf16[768,256]{1,0:T(8,128)(2,1)} %param.32) | copy-start | bytes 1179652
  278.3 15.0 %collective-permute-start.8 = (f32[192,384]{1,0:T(8,128)S(1)}, f32[192,384]{1,0:T(8,128)S(1)}, u32[]{:S(2)}, u32[]{:S(2)}) collective-permute-start(f32[192,384]{1,0:T(8,128)S(1)} %bitcast.101), channel_id=1, source_target_pairs={{0,8},{1,9},{2,10},{3,11},{4,12},{5,13},{6,14},{7,15},{8,0},{9,1},... | collective-permute-start | bytes 884744 | tf_op jit(solution)/shard_map/ppermute | solution.py:277
  288.7 11.2 %collective-permute-start.4 = (f32[96,384]{1,0:T(8,128)S(1)}, f32[96,384]{1,0:T(8,128)S(1)}, u32[]{:S(2)}, u32[]{:S(2)}) collective-permute-start(f32[96,384]{1,0:T(8,128)S(1)} %dynamic-slice_bitcast_fusion.1), channel_id=1, source_target_pairs={{0,16},{1,17},{2,18},{3,19},{4,20},{5,21},{6,22},{7,23},{8,24},{9,... | collective-permute-start | bytes 442376 | tf_op jit(solution)/shard_map/ppermute | solution.py:277
  293.4 8.2 %collective-permute-start.9 = (f32[96,384]{1,0:T(8,128)S(1)}, f32[96,384]{1,0:T(8,128)S(1)}, u32[]{:S(2)}, u32[]{:S(2)}) collective-permute-start(f32[96,384]{1,0:T(8,128)S(1)} %dynamic-slice_bitcast_fusion), channel_id=1, source_target_pairs={{0,16},{1,17},{2,18},{3,19},{4,20},{5,21},{6,22},{7,23},{8,24},{9,... | collective-permute-start | bytes 442376 | tf_op jit(solution)/shard_map/ppermute | solution.py:277

commit v2 on v1

--- a/solution.py
+++ b/solution.py
@@ -28,7 +28,7 @@
     return [pl.BlockSpec(memory_space=pltpu.VMEM)] * count
 
 
-def prepare_kernel(x_ref, k_ref, bias_ref, gain_ref, shift_ref, normed_ref, hat_ref, rstd_ref, fsum_ref, xs, ks):
+def prepare_kernel(x_ref, k_ref, vec_ref, normed_ref, hat_ref, rstd_ref, fsum_ref, xs, ks):
     tiles, channels = x_ref.shape[1], x_ref.shape[2]
     ks[...] = k_ref[...].astype(jnp.float32)
 
@@ -40,7 +40,7 @@
             xs[p] = value
             total = total + value
         fsum_ref[:, lanes] = total
-        bias = jnp.broadcast_to(bias_ref[:, lanes].astype(jnp.float32), (tiles, LANES))
+        bias = jnp.broadcast_to(vec_ref[0:1, lanes], (tiles, LANES))
         for i in range(SIDE):
             accs = [bias for _ in range(SIDE)]
             for a in range(KERNEL):
@@ -60,8 +60,8 @@
         return carry
 
     lax.fori_loop(0, channels // LANES, block, 0)
-    gain = gain_ref[...].astype(jnp.float32)
-    shift = shift_ref[...].astype(jnp.float32)
+    gain = vec_ref[1:2, :]
+    shift = vec_ref[2:3, :]
 
     def norm(p, carry):
         rows = pl.ds(pl.multiple_of(p * tiles, tiles), tiles)
@@ -78,7 +78,7 @@
     lax.fori_loop(0, POSITIONS, norm, 0, unroll=7)
 
 
-def prepare(x, kernel, bias, gain, shift):
+def prepare(x, kernel, vectors):
     positions, tiles, channels = x.shape
     rows = positions * tiles
     return pl.pallas_call(
@@ -89,7 +89,7 @@
             jax.ShapeDtypeStruct((rows, LANES), jnp.float32),
             jax.ShapeDtypeStruct((tiles, channels), jnp.float32),
         ),
-        in_specs=whole_vmem(5),
+        in_specs=whole_vmem(3),
         out_specs=tuple(whole_vmem(4)),
         scratch_shapes=[
             pltpu.VMEM((positions, tiles, LANES), jnp.float32),
@@ -97,10 +97,7 @@
         ],
         compiler_params=pltpu.CompilerParams(vmem_limit_bytes=VMEM_LIMIT),
         cost_estimate=pl.CostEstimate(flops=40_000_000, bytes_accessed=5_000_000, transcendentals=0),
-    )(x, kernel, bias, gain, shift)
-
-
-ROWS_STEP = 112
+    )(x, kernel, vectors)
 
 
 def hidden_kernel(normed_ref, w_ref, bias_ref, pooled_ref, slope_ref, hid):
@@ -156,7 +153,7 @@
     )(normed, w_in, in_bias)
 
 
-def grad_hidden_kernel(slope_ref, ga_ref, normed_ref, gh_ref, gw_ref, gb_ref):
+def grad_hidden_kernel(slope_ref, ga_ref, normed_ref, gh_ref, first_ref, second_ref, gb_ref):
     rows = slope_ref.shape[0]
     tiles, width = ga_ref.shape
     for c in range(width // LANES):
@@ -173,9 +170,12 @@
             0, rows // tiles, step, jnp.zeros((tiles, LANES), jnp.float32), unroll=7
         )
         gb_ref[:, lanes] = jnp.sum(total, axis=0, keepdims=True)
-    gw_ref[...] = lax.dot_general(
+    whole = lax.dot_general(
         gh_ref[...], normed_ref[...], (((0,), (0,)), ((), ())), preferred_element_type=jnp.float32
     )
+    half = first_ref.shape[1]
+    first_ref[...] = whole[:, :half]
+    second_ref[...] = whole[:, half:]
 
 
 def grad_hidden_layer(slope, grad_active, normed):
@@ -188,7 +188,8 @@
         grid=(ff // width,),
         out_shape=(
             jax.ShapeDtypeStruct((rows, ff), jnp.bfloat16),
-            jax.ShapeDtypeStruct((ff, channels), jnp.float32),
+            jax.ShapeDtypeStruct((ff, channels // 2), jnp.float32),
+            jax.ShapeDtypeStruct((ff, channels // 2), jnp.float32),
             jax.ShapeDtypeStruct((1, ff), jnp.float32),
         ),
         in_specs=[
@@ -198,7 +199,8 @@
         ],
         out_specs=(
             pl.BlockSpec((rows, width), lambda f: (0, f)),
-            pl.BlockSpec((width, channels), lambda f: (f, 0)),
+            pl.BlockSpec((width, channels // 2), lambda f: (f, 0)),
+            pl.BlockSpec((width, channels // 2), lambda f: (f, 0)),
             pl.BlockSpec((1, width), lambda f: (0, f)),
         ),
         compiler_params=pltpu.CompilerParams(vmem_limit_bytes=VMEM_LIMIT),
@@ -208,9 +210,9 @@
     )(slope, grad_active, normed)
 
 
-def prepare_back_kernel(gn_ref, hat_ref, rstd_ref, x_ref, gain_ref, out_ref, gc, xs):
+def prepare_back_kernel(gn_ref, hat_ref, rstd_ref, x_ref, vec_ref, out_ref, gc, xs):
     tiles, channels = x_ref.shape[1], x_ref.shape[2]
-    gain = gain_ref[...].astype(jnp.float32)
+    gain = vec_ref[1:2, :]
 
     def norm(p, carry):
         total_gain, total_shift = carry
@@ -256,7 +258,7 @@
     lax.fori_loop(0, channels // LANES, block, 0)
 
 
-def prepare_back(grad_normed, hat, rstd, x, gain):
+def prepare_back(grad_normed, hat, rstd, x, vectors):
     positions, tiles, channels = x.shape
     return pl.pallas_call(
         prepare_back_kernel,
@@ -269,7 +271,7 @@
         ],
         compiler_params=pltpu.CompilerParams(vmem_limit_bytes=VMEM_LIMIT),
         cost_estimate=pl.CostEstimate(flops=40_000_000, bytes_accessed=8_000_000, transcendentals=0),
-    )(grad_normed, hat, rstd, x, gain)
+    )(grad_normed, hat, rstd, x, vectors)
 
 
 def swap(values, bit, devices):
@@ -296,6 +298,99 @@
     return current
 
 
+def exchange_kernel(
+    devices, n_slide, sums_ref, pooled_ref, grad_ref, head_ref,
+    total_ref, all_pooled_ref, all_grad_ref, all_head_ref, landed, send_sem, recv_sem,
+):
+    me = lax.axis_index("enc") * n_slide + lax.axis_index("slide")
+
+    def place(device):
+        return {"enc": device // n_slide, "slide": lax.rem(device, n_slide)}
+
+    def each(body):
+        def step(k, carry):
+            body(k, lax.rem(me + k, devices), lax.rem(me + devices - k, devices))
+            return carry
+
+        lax.fori_loop(1, devices, step, 0)
+
+    def copy(kind, k, source, target, device):
+        return pltpu.make_async_remote_copy(
+            src_ref=source, dst_ref=target, send_sem=send_sem.at[kind, k],
+            recv_sem=recv_sem.at[kind, k], device_id=place(device),
+            device_id_type=pl.DeviceIdType.MESH,
+        )
+
+    barrier = pltpu.get_barrier_semaphore()
+    each(lambda k, to, source: pl.semaphore_signal(
+        barrier, inc=1, device_id=place(to), device_id_type=pl.DeviceIdType.MESH))
+    pl.semaphore_wait(barrier, devices - 1)
+
+    def sums(k, to, slot):
+        return copy(0, k, sums_ref.at[to], landed.at[slot], to)
+
+    def others(k, to, slot):
+        return (
+            copy(1, k, pooled_ref.at[to], all_pooled_ref.at[slot], to),
+            copy(2, k, grad_ref, all_grad_ref.at[slot], to),
+            copy(3, k, head_ref, all_head_ref.at[slot], to),
+        )
+
+    def totals(k, to, slot):
+        return copy(4, k, total_ref.at[me], total_ref.at[slot], to)
+
+    each(lambda k, to, source: sums(k, to, me).start())
+    landed[me] = sums_ref[me]
+    all_pooled_ref[me] = pooled_ref[me]
+    all_grad_ref[me] = grad_ref[...]
+    all_head_ref[me] = head_ref[...]
+
+    def start_others(k, to, source):
+        for item in others(k, to, me):
+            item.start()
+
+    each(start_others)
+    each(lambda k, to, source: sums(k, to, source).wait_recv())
+    total_ref[me] = jnp.sum(landed[...], axis=0)
+    each(lambda k, to, source: totals(k, to, me).start())
+
+    def finish(k, to, source):
+        sums(k, to, me).wait_send()
+        for item in others(k, to, source):
+            item.wait_recv()
+        for item in others(k, to, me):
+            item.wait_send()
+        totals(k, to, source).wait_recv()
+        totals(k, to, me).wait_send()
+
+    each(finish)
+
+
+def exchange(devices, n_slide, sums, pooled, grad, head):
+    return pl.pallas_call(
+        partial(exchange_kernel, devices, n_slide),
+        out_shape=(
+            jax.ShapeDtypeStruct(sums.shape, sums.dtype),
+            jax.ShapeDtypeStruct(pooled.shape, pooled.dtype),
+            jax.ShapeDtypeStruct((devices,) + grad.shape, grad.dtype),
+            jax.ShapeDtypeStruct((devices,) + head.shape, head.dtype),
+        ),
+        in_specs=whole_vmem(4),
+        out_specs=tuple(whole_vmem(4)),
+        scratch_shapes=[
+            pltpu.VMEM(sums.shape, sums.dtype),
+            pltpu.SemaphoreType.DMA((5, devices)),
+            pltpu.SemaphoreType.DMA((5, devices)),
+        ],
+        compiler_params=pltpu.CompilerParams(
+            collective_id=0, has_side_effects=True, vmem_limit_bytes=VMEM_LIMIT
+        ),
+        cost_estimate=pl.CostEstimate(
+            flops=1_000_000, bytes_accessed=40_000_000, transcendentals=0
+        ),
+    )(sums, pooled, grad, head)
+
+
 def per_device(
     tile_features, tile_slide, slide_order, targets, dw_kernel, dw_bias, norm_gain, norm_bias,
     w_in, in_bias, w_out, out_bias, layer_scale, final_gain, final_bias, head_weight, head_bias,
@@ -314,18 +409,12 @@
     index = enc_index * n_slide + slide_index
 
     hot = (tile_slide == slide_order).astype(f32)
-    tally = jnp.pad(jnp.sum(hot, axis=0)[None, :], ((0, 0), (0, -slides % genes)))
-    early = lax.all_gather(
-        jnp.concatenate([targets[0], tally.reshape(-1, genes)], axis=0), "slide"
-    )
-    all_targets = early[:, :owned].reshape(slides, genes)
-    counts = jnp.sum(early[:, owned:].reshape(n_slide, -1), axis=0)[:slides]
-    divisor = jnp.maximum(counts, 1.0)[:, None]
+    early = jnp.concatenate([targets.reshape(-1), jnp.sum(hot, axis=0)])
+    early = jnp.pad(early, (0, -early.shape[0] % channels)).reshape(-1, channels)
 
     x = jnp.transpose(tile_features, (1, 2, 0, 3)).reshape(POSITIONS, tiles, channels)
-    normed, hat, rstd, feature_sum = prepare(
-        x, dw_kernel, dw_bias[None, :], norm_gain[None, :], norm_bias[None, :]
-    )
+    vectors = jnp.stack([dw_bias, norm_gain, norm_bias]).astype(f32)
+    normed, hat, rstd, feature_sum = prepare(x, dw_kernel, vectors)
     pooled_active, slope = hidden_layer(normed, w_in, in_bias[None, :], tiles)
     high = lax.reduce_precision(pooled_active, 8, 7)
     both = jnp.concatenate([high, pooled_active - high], axis=0).astype(bf16)
@@ -340,7 +429,12 @@
         hot.astype(bf16), embedded.astype(bf16), (((0,), (0,)), ((), ())),
         preferred_element_type=f32,
     )
-    slide_mean = jnp.sum(lax.all_gather(partial_sums, "slide"), axis=0) / divisor
+    group = lax.all_gather(jnp.concatenate([partial_sums, early], axis=0), "slide")
+    early = group[:, slides:].reshape(n_slide, -1)
+    all_targets = early[:, : owned * genes].reshape(slides, genes)
+    counts = jnp.sum(early[:, owned * genes : owned * genes + slides], axis=0)
+    divisor = jnp.maximum(counts, 1.0)[:, None]
+    slide_mean = jnp.sum(group[:, :slides], axis=0) / divisor
     head_wide = head_weight.astype(f32)
     prediction = jnp.dot(
         slide_mean, head_wide, precision=highest, preferred_element_type=f32
@@ -363,24 +457,19 @@
     grad_active = lax.dot_general(
         grad_projected, w_out, (((1,), (1,)), ((), ())), preferred_element_type=f32
     )
-    grad_hidden, partial_w_in, grad_inner = grad_hidden_layer(slope, grad_active, normed)
+    grad_hidden, first, second, grad_inner = grad_hidden_layer(slope, grad_active, normed)
 
     bits = devices.bit_length() - 1
     inner = n_slide.bit_length() - 1
     xs = list(range(1, inner))
     rest = list(range(inner, bits))
-    half = channels // 2
     narrow = (1, inner)
-    first = halve_scatter(
-        partial_w_in[:, :half], [0] + xs + rest, narrow, devices, index
-    )
-    second = halve_scatter(
-        partial_w_in[:, half:], [0] + rest[:1] + xs + rest[1:], narrow, devices, index
-    )
+    first = halve_scatter(first, [0] + xs + rest, narrow, devices, index)
+    second = halve_scatter(second, [0] + rest[:1] + xs + rest[1:], narrow, devices, index)
     grad_w_in = jnp.concatenate([first, second], axis=1)
 
     grad_normed = jnp.dot(grad_hidden, w_in, preferred_element_type=f32)
-    small = prepare_back(grad_normed, hat, rstd, x, norm_gain[None, :])
+    small = prepare_back(grad_normed, hat, rstd, x, vectors)
     bundle = jnp.concatenate(
         [
             small, grad_out_bias[None], grad_scale[None], grad_fgain[None], grad_fbias[None],
@@ -389,25 +478,24 @@
         axis=0,
     )
     used = bundle.shape[0]
-    bundle = jnp.pad(bundle, ((0, -used % 64), (0, 0)))
-    lines = bundle.reshape(devices, -1)
-    lines = lax.all_to_all(lines, AXES, split_axis=0, concat_axis=0, tiled=True)
-    bundle = lax.all_gather(jnp.sum(lines, axis=0), AXES).reshape(-1, channels)
-
-    head_parts = lax.all_gather(
-        jnp.concatenate([slide_mean, grad_pred], axis=1), "enc"
-    ).reshape(n_enc * slides, channels + genes)
+    bundle = jnp.pad(bundle, ((0, -used % devices), (0, 0))).reshape(devices, -1, channels)
+    mine = pooled_active.reshape(tiles, devices, ff // devices).transpose(1, 0, 2)
+    head_rows = lax.dynamic_slice_in_dim(
+        jnp.concatenate([slide_mean, grad_pred], axis=1), slide_index * owned, owned
+    )
+    bundle, mine, all_grad, head_parts = exchange(
+        devices, n_slide, bundle, mine, grad_projected, head_rows
+    )
+    bundle = bundle.reshape(-1, channels)
+    head_parts = head_parts.reshape(-1, channels + genes)
     grad_head_w = lax.dot_general(
         head_parts[:, :channels], head_parts[:, channels:], (((0,), (0,)), ((), ())),
         precision=highest, preferred_element_type=f32,
     )
     grad_head_b = jnp.sum(head_parts[:, channels:], axis=0)
-
-    mine = pooled_active.reshape(tiles, devices, ff // devices).transpose(1, 0, 2)
-    mine = lax.all_to_all(mine, AXES, split_axis=0, concat_axis=0, tiled=True)
     mine = mine.reshape(devices * tiles, ff // devices)
     mine_high = lax.reduce_precision(mine, 8, 7)
-    all_grad = lax.all_gather(grad_projected, AXES, tiled=True)
+    all_grad = all_grad.reshape(devices * tiles, channels)
 
     def rows_product(left):
         return lax.dot_general(

time: 303 us -> 212 us (0.70)
  blocking collectives: 129 us -> 7.02 us
  Pallas kernels: 61.3 us -> 110 us
  local copies, waits for them, and re-layouts: 23.6 us -> 16.8 us
  starting transfers between devices: 14.5 us -> 8.57 us
  waiting for transfers between devices: 42 us -> 38.1 us
    all_gather x5 -> x1, blocking collectives: 129 us -> 7.02 us  [per_device(): lax.all_gather(jnp.concatenate([partial_sums, early], axis=0), 'slide')]
    pallas_call x0 -> x1, Pallas kernels: none -> 49.1 us  [exchange(): pl.pallas_call(partial(exchange_kernel, devices, n_slide), out_shape=(jax...]
    all_to_all x2 -> x0, starting transfers between devices: 9.72 us -> none  [the longest x1 6.23 us: per_device(): lines = lax.all_to_all(lines, AXES, split_axis=0, concat_axis=0, tiled=True)]
    slice x3 -> x2, local copies, waits for them, and re-layouts: 8.01 us -> 0.01 us  [the longest x1 0.01 us: per_device(): early = group[:, slides:].reshape(n_slide, -1)]
    ppermute x10, waiting for transfers between devices: 42 us -> 38.1 us  [swap(): return lax.ppermute(values, AXES, pairs)]
    broadcast_in_dim x3 -> x0, local copies, waits for them, and re-layouts: 3.79 us -> none  [the longest x1 1.26 us: per_device(): norm_gain[None, :]]
    ppermute x10, starting transfers between devices: 4.81 us -> 8.57 us  [swap(): return lax.ppermute(values, AXES, pairs)]
    reshape x1 -> x6, local copies, waits for them, and re-layouts: 0.01 us -> 3.61 us  [the longest x1 1.13 us: per_device(): head_parts = head_parts.reshape(-1, channels + genes)]
  transfers between devices with their start and end apart: 12 -> 10, of which waited for: 8 -> 8; matrix products, arithmetic and copies ran while one was open for 8% -> 12% of each run, Pallas kernels for 5% -> 31%
where the time goes in v2:
time: 212 us
  Pallas kernels  110 us (52%)
  waiting for transfers between devices  38.1 us (18%)
  matrix products  20 us (9%)
  local copies, waits for them, and re-layouts  16.8 us (8%)
  other arithmetic  10.1 us (5%)
  starting transfers between devices  8.57 us (4%)
  blocking collectives  7.02 us (3%)
    pallas_call x1, Pallas kernels, exchange(): pl.pallas_call(partial(exchange_kernel, devices, n_slide), out_shape=(jax...  49.1 us
    ppermute x10, waiting for transfers between devices, swap(): return lax.ppermute(values, AXES, pairs)  38.1 us
    pallas_call x1, Pallas kernels, prepare(): pl.pallas_call(prepare_kernel, out_shape=(jax.ShapeDtypeStruct((rows, cha...  17.6 us
    pallas_call x1, Pallas kernels, prepare_back(): pl.pallas_call(prepare_back_kernel, out_shape=jax.ShapeDtypeStruct((posit...  15.7 us
    pallas_call x1, Pallas kernels, hidden_layer(): pl.pallas_call(hidden_kernel, grid=(ff // width,), out_shape=(jax.ShapeDt...  14.1 us
    pallas_call x1, Pallas kernels, grad_hidden_layer(): pl.pallas_call(grad_hidden_kernel, grid=(ff // width,), out_shape=(jax.Sh...  13.5 us
    dot_general x1, matrix products, per_device(): grad_normed = jnp.dot(grad_hidden, w_in, preferred_element_type=f32)  9.13 us
    ppermute x10, starting transfers between devices, swap(): return lax.ppermute(values, AXES, pairs)  8.57 us
  transfers between devices with their start and end apart: 10, of which 8 were waited for; matrix products, arithmetic and copies ran while one was open for 12% of the time, Pallas kernels for 31%

profile of v2, /device:TPU:0, one launch (start us, length us, event | category | flops | bytes accessed | tf_op | source)
XLA Modules:
  0.0 211.7 jit_solution(1813591157215969724)
XLA Ops:
  0.6 0.7 stack.12
  1.4 0.7 stack.13
  2.1 0.7 stack.14
  2.8 1.3 broadcast_in_dim.12.bias_ref
  4.1 0.6 maximum_convert_fusion.vec_ref
  4.7 17.6 %shard_map.224 = (bf16[784,768]{1,0:T(8,128)(2,1)}, f32[784,768]{1,0:T(8,128)}, f32[784,128]{1,0:T(8,128)}, f32[16,768]{1,0:T(8,128)}) custom-call(bf16[49,16,768]{2,1,0:T(8,128)(2,1)} %bitcast.82, bf16[49,768]{1,0:T(8,128)(2,1)} %k_ref.1, f32[3,768]{1,0:T(4,128)} %maximum_convert_fusion.vec_ref), custom_call_target="tpu_custom_call" | custom-call | flops 40000000 | bytes 5000000 | tf_op jit(solution)/shard_map/pallas_call | solution.py:84
  22.3 14.1 %shard_map.225 = (f32[16,3072]{1,0:T(8,128)}, f32[784,3072]{1,0:T(8,128)}) custom-call(bf16[784,768]{1,0:T(8,128)(2,1)} %get-tuple-element.22.normed_ref, bf16[3072,768]{1,0:T(8,128)(2,1)} %w_ref.1, bf16[1,3072]{1,0:T(2,128)(2,1)} %broadcast_in_dim.12.bias_ref), custom_call_target="tpu_custom_call" | custom-call | flops 3699376128 | bytes 20000000 | tf_op jit(solution)/shard_map/pallas_call | solution.py:132
  36.4 0.9 reduce-precision_convert_fusion.1
  37.5 0.9 fusion.7
  39.2 7.0 %all-gather.1 = f32[4,9,768]{2,1,0:T(8,128)S(1)} all-gather(f32[1,9,768]{2,1,0:T(8,128)S(1)} %maximum_bitcast_fusion), channel_id=2, replica_groups=mesh['enc'=8,'slide'=4] {'slide'}, dimensions={0}, use_global_device_ids=true | all-gather | bytes 138240 | tf_op jit(solution)/shard_map/all_gather | solution.py:432
  48.0 4.4 %fusion.30.ga_ref = f32[16,3072]{1,0:T(8,128)} fusion(bf16[16,768]{1,0:T(8,128)(2,1)S(1)} %get-tuple-element.47.grad_ref, bf16[3072,768]{1,0:T(8,128)(2,1)} %param.27), kind=kOutput, calls=%fused_computation.91 | convolution fusion | flops 75497472 | bytes 4939776 | tf_op jit(solution)/shard_map/dot_general | solution.py:457
  52.3 13.5 %shard_map.226 = (bf16[784,3072]{1,0:T(8,128)(2,1)}, f32[3072,384]{1,0:T(8,128)}, f32[3072,384]{1,0:T(8,128)}, f32[1,3072]{1,0:T(1,128)}) custom-call(f32[784,3072]{1,0:T(8,128)} %get-tuple-element.23.slope_ref, f32[16,3072]{1,0:T(8,128)} %fusion.30.ga_ref, bf16[784,768]{1,0:T(8,128)(2,1)} %get-tuple-element.22.normed_ref), custom_call_target="tpu_custom_call" | custom-call | flops 3699376128 | bytes 25000000 | tf_op jit(solution)/shard_map/pallas_call | solution.py:186
  65.8 2.0 constant_dynamic-slice_fusion.3
  68.3 0.6 copy-done.2
  68.9 1.6 constant_dynamic-slice_fusion.1
  71.5 0.7 reduce.3
  72.3 9.1 %fusion.31.gn_ref = f32[784,768]{1,0:T(8,128)} fusion(bf16[784,3072]{1,0:T(8,128)(2,1)} %get-tuple-element.28, bf16[3072,768]{1,0:T(8,128)(2,1)} %w_ref.1), kind=kOutput, calls=%fused_computation.92 | convolution fusion | flops 3699376128 | bytes 11943936 | tf_op jit(solution)/shard_map/dot_general | solution.py:471
  81.4 15.7 %shard_map.227 = f32[52,768]{1,0:T(8,128)} custom-call(f32[784,768]{1,0:T(8,128)} %fusion.31.gn_ref, f32[784,768]{1,0:T(8,128)} %get-tuple-element.29.hat_ref, f32[784,128]{1,0:T(8,128)} %get-tuple-element.30.rstd_ref, bf16[49,16,768]{2,1,0:T(8,128)(2,1)} %bitcast.83, f32[3,768]{1,0:T(4,128)} %maximum_convert_fusion.vec_ref), custom_call_target="tpu_custom_call" | custom-call | flops 40000000 | bytes 8000000 | tf_op jit(solution)/shard_map/pallas_call | solution.py:263
  97.2 1.0 concatenate.23
  98.2 0.8 reshape.173.sums_ref
  98.9 0.9 copy.45
  99.8 0.6 fusion.20.head_ref
  100.4 49.1 %shard_map.228 = (f32[32,2,768]{2,1,0:T(2,128)}, f32[32,16,96]{2,1,0:T(8,128)}, bf16[32,16,768]{2,1,0:T(8,128)(2,1)}, f32[32,2,1024]{2,1,0:T(2,128)}) custom-call(f32[32,2,768]{2,1,0:T(2,128)} %reshape.173.sums_ref, f32[32,16,96]{2,1,0:T(8,128)} %bitcast.89, bf16[16,768]{1,0:T(8,128)(2,1)} %copy-done.6, f32[2,1024]{1,0:T(2,128)} %fusion.20.head_ref), custom_call_target="tpu_custom_call" | custom-call | flops 1000000 | bytes 40000000 | tf_op jit(solution)/shard_map/pallas_call | solution.py:370
  149.5 1.1 reshape.175
  150.5 0.7 slice.52
  151.2 0.6 slice.53
  151.8 0.7 slice.43
  152.6 1.1 reshape.177
  153.7 0.6 reshape.176
  154.3 0.6 dynamic-slice_bitcast_fusion.2
  154.9 0.6 slice_reduce_fusion.1
  155.5 1.5 convolution_bitcast_fusion
  157.0 4.4 %bitcast_add_fusion = (f32[2,2,2,2,96,384]{5,4,3,2,1,0:T(8,128)S(1)}, f32[2,2,2,2,96,384]{5,4,3,2,1,0:T(8,128)S(1)}) fusion(f32[2,2,2,2,96,384]{5,4,3,2,1,0:T(8,128)} %bitcast.23, f32[2,2,2,2,2,96,384]{6,5,4,3,2,1,0:T(8,128)} %bitcast.86, s32[]{:T(128)S(6)} %select_n.50, f32[2,2,2,2,96,384]{5,4,3,2,1,0:T(8,128)} %bitcast.8, ...), kind=kLoop, calls=%fused_computation | loop fusion | flops 1179648 | bytes 14155780 | tf_op jit(solution)/shard_map/add | solution.py:297
  161.5 1.8 collective-permute-start.1
  163.3 1.0 fusion
  164.4 1.1 collective-permute-start.6
  165.5 1.7 fusion.5
  167.2 9.8 %collective-permute-done.1 = bf16[768,384]{1,0:T(8,128)(2,1)S(1)} collective-permute-done((bf16[768,384]{1,0:T(8,128)(2,1)S(1)}, bf16[768,384]{1,0:T(8,128)(2,1)S(1)}, u32[]{:S(2)}, u32[]{:S(2)}) %collective-permute-start.1) | collective-permute-done | bytes 589856 | tf_op jit(solution)/shard_map/ppermute | solution.py:279
  177.1 1.1 collective-permute-start.2
  178.2 1.6 collective-permute-done.6
  180.2 5.6 %collective-permute-done.2 = bf16[384,384]{1,0:T(8,128)(2,1)S(1)} collective-permute-done((bf16[384,384]{1,0:T(8,128)(2,1)S(1)}, bf16[384,384]{1,0:T(8,128)(2,1)S(1)}, u32[]{:S(2)}, u32[]{:S(2)}) %collective-permute-start.2) | collective-permute-done | bytes 294944 | tf_op jit(solution)/shard_map/ppermute | solution.py:279
  185.9 1.6 collective-permute-start.3
  187.7 1.6 collective-permute-start.8
  189.3 8.2 %collective-permute-done.3 = f32[192,384]{1,0:T(8,128)S(1)} collective-permute-done((f32[192,384]{1,0:T(8,128)S(1)}, f32[192,384]{1,0:T(8,128)S(1)}, u32[]{:S(2)}, u32[]{:S(2)}) %collective-permute-start.3) | collective-permute-done | bytes 294944 | tf_op jit(solution)/shard_map/ppermute | solution.py:279
  197.6 3.9 %collective-permute-done.8 = f32[192,384]{1,0:T(8,128)S(1)} collective-permute-done((f32[192,384]{1,0:T(8,128)S(1)}, f32[192,384]{1,0:T(8,128)S(1)}, u32[]{:S(2)}, u32[]{:S(2)}) %collective-permute-start.8) | collective-permute-done | bytes 294944 | tf_op jit(solution)/shard_map/ppermute | solution.py:279
  202.1 5.5 %collective-permute-done.4 = f32[96,384]{1,0:T(8,128)S(1)} collective-permute-done((f32[96,384]{1,0:T(8,128)S(1)}, f32[96,384]{1,0:T(8,128)S(1)}, u32[]{:S(2)}, u32[]{:S(2)}) %collective-permute-start.4) | collective-permute-done | bytes 147488 | tf_op jit(solution)/shard_map/ppermute | solution.py:279
  207.7 3.2 %collective-permute-done.9 = f32[96,384]{1,0:T(8,128)S(1)} collective-permute-done((f32[96,384]{1,0:T(8,128)S(1)}, f32[96,384]{1,0:T(8,128)S(1)}, u32[]{:S(2)}, u32[]{:S(2)}) %collective-permute-start.9) | collective-permute-done | bytes 147488 | tf_op jit(solution)/shard_map/ppermute | solution.py:279
  210.9 0.7 pad_maximum_fusion
  (101 shorter events, 5.7 us)
Async XLA Ops:
  0.6 45.8 %copy-start = (bf16[768,256]{1,0:T(8,128)(2,1)S(1)}, bf16[768,256]{1,0:T(8,128)(2,1)}, u32[]{:S(2)}) copy-start(bf16[768,256]{1,0:T(8,128)(2,1)} %param.32) | copy-start | bytes 1179652
  4.7 32.7 %slice-start = ((s8[4718592]{0:T(1024)(128)(4,1)}), s8[4194304]{0:T(1024)(128)(4,1)S(1)}, s32[]{:S(2)}) async-start(s8[4718592]{0:T(1024)(128)(4,1)} %bitcast.80), calls=%async_computation | async-start | bytes 8388608
  22.3 15.0 %copy-start.9 = (bf16[768]{0:T(1024)(128)(2,1)S(1)}, bf16[768]{0:T(1024)(128)(2,1)}, u32[]{:S(2)}) copy-start(bf16[768]{0:T(1024)(128)(2,1)} %param.29) | copy-start | bytes 4612
  22.3 15.0 %copy-start.10 = (bf16[768]{0:T(1024)(128)(2,1)S(1)}, bf16[768]{0:T(1024)(128)(2,1)}, u32[]{:S(2)}) copy-start(bf16[768]{0:T(1024)(128)(2,1)} %param.28) | copy-start | bytes 4612
  22.3 15.1 %slice-start.1 = ((s8[4718592]{0:T(1024)(128)(4,1)}), s8[524288]{0:T(1024)(128)(4,1)S(1)}, s32[]{:S(2)}) async-start(s8[4718592]{0:T(1024)(128)(4,1)} %bitcast.80), calls=%async_computation.1 | async-start | bytes 1048576
  37.4 0.9 copy-start.7
  37.4 1.3 copy-start.11
  37.4 1.3 copy-start.12
  37.4 1.3 copy-start.13
  37.4 1.3 copy-start.15
  37.5 1.3 copy-start.16
  37.5 8.8 %copy-start.14 = (bf16[256]{0:T(256)(128)(2,1)S(1)}, bf16[256]{0:T(256)(128)(2,1)}, u32[]{:S(2)}) copy-start(bf16[256]{0:T(256)(128)(2,1)} %param.33) | copy-start | bytes 1540
  48.0 4.4 %copy-start.6 = (bf16[16,768]{1,0:T(8,128)(2,1)}, bf16[16,768]{1,0:T(8,128)(2,1)S(1)}, u32[]{:S(2)}) copy-start(bf16[16,768]{1,0:T(8,128)(2,1)S(1)} %get-tuple-element.47.grad_ref) | copy-start | bytes 73732
  65.8 3.0 %copy-start.2 = (f32[3072,384]{1,0:T(8,128)S(1)}, f32[3072,384]{1,0:T(8,128)}, u32[]{:S(2)}) copy-start(f32[3072,384]{1,0:T(8,128)} %get-tuple-element.27) | copy-start | bytes 14155780
  67.9 89.1 %collective-permute-start = (f32[1536,384]{1,0:T(8,128)S(1)}, f32[1536,384]{1,0:T(8,128)}, u32[]{:S(2)}, u32[]{:S(2)}) collective-permute-start(f32[1536,384]{1,0:T(8,128)S(1)} %bitcast.88), channel_id=1, source_target_pairs={{0,1},{1,0},{2,3},{3,2},{4,5},{5,4},{6,7},{7,6},{8,9},{9,8},{10,11... | collective-permute-start | bytes 7077896 | tf_op jit(solution)/shard_map/ppermute | solution.py:279
  68.9 2.0 copy-start.5
  68.9 2.6 %copy-start.8 = (f32[1,3072]{1,0:T(1,128)S(1)}, f32[1,3072]{1,0:T(1,128)}, u32[]{:S(2)}) copy-start(f32[1,3072]{1,0:T(1,128)} %get-tuple-element.31) | copy-start | bytes 36868
  70.5 86.5 %collective-permute-start.5 = (f32[1536,384]{1,0:T(8,128)}, f32[1536,384]{1,0:T(8,128)}, u32[]{:S(2)}, u32[]{:S(2)}) collective-permute-start(f32[1536,384]{1,0:T(8,128)} %bitcast.22), channel_id=1, source_target_pairs={{0,1},{1,0},{2,3},{3,2},{4,5},{5,4},{6,7},{7,6},{8,9},{9,8},{10,11... | collective-permute-start | bytes 7077896 | tf_op jit(solution)/shard_map/ppermute | solution.py:279
  157.0 6.3 %copy-start.3 = (bf16[32,16,768]{2,1,0:T(8,128)(2,1)S(1)}, bf16[32,16,768]{2,1,0:T(8,128)(2,1)}, u32[]{:S(2)}) copy-start(bf16[32,16,768]{2,1,0:T(8,128)(2,1)} %get-tuple-element.33) | copy-start | bytes 2359300
  157.0 6.3 %copy-start.4 = (f32[32,16,96]{2,1,0:T(8,128)S(1)}, f32[32,16,96]{2,1,0:T(8,128)}, u32[]{:S(2)}) copy-start(f32[32,16,96]{2,1,0:T(8,128)} %get-tuple-element.32) | copy-start | bytes 589828
  161.5 15.4 %collective-permute-start.1 = (bf16[768,384]{1,0:T(8,128)(2,1)S(1)}, bf16[768,384]{1,0:T(8,128)(2,1)S(1)}, u32[]{:S(2)}, u32[]{:S(2)}) collective-permute-start(bf16[768,384]{1,0:T(8,128)(2,1)S(1)} %bitcast.91), channel_id=1, source_target_pairs={{0,2},{1,3},{2,0},{3,1},{4,6},{5,7},{6,4},{7,5},{8,10},{9,11},{10,... | collective-permute-start | bytes 1769480 | tf_op jit(solution)/shard_map/ppermute | solution.py:279
  164.4 15.5 %collective-permute-start.6 = (bf16[768,384]{1,0:T(8,128)(2,1)S(1)}, bf16[768,384]{1,0:T(8,128)(2,1)S(1)}, u32[]{:S(2)}, u32[]{:S(2)}) collective-permute-start(bf16[768,384]{1,0:T(8,128)(2,1)S(1)} %bitcast.90), channel_id=1, source_target_pairs={{0,4},{1,5},{2,6},{3,7},{4,0},{5,1},{6,2},{7,3},{8,12},{9,13},{10,... | collective-permute-start | bytes 1769480 | tf_op jit(solution)/shard_map/ppermute | solution.py:279
  177.1 8.7 %collective-permute-start.2 = (bf16[384,384]{1,0:T(8,128)(2,1)S(1)}, bf16[384,384]{1,0:T(8,128)(2,1)S(1)}, u32[]{:S(2)}, u32[]{:S(2)}) collective-permute-start(bf16[384,384]{1,0:T(8,128)(2,1)S(1)} %bitcast.96), channel_id=1, source_target_pairs={{0,4},{1,5},{2,6},{3,7},{4,0},{5,1},{6,2},{7,3},{8,12},{9,13},{10,... | collective-permute-start | bytes 884744 | tf_op jit(solution)/shard_map/ppermute | solution.py:279
  180.1 7.6 %collective-permute-start.7 = (bf16[384,384]{1,0:T(8,128)(2,1)S(1)}, bf16[384,384]{1,0:T(8,128)(2,1)S(1)}, u32[]{:S(2)}, u32[]{:S(2)}) collective-permute-start(bf16[384,384]{1,0:T(8,128)(2,1)S(1)} %bitcast.97), channel_id=1, source_target_pairs={{0,2},{1,3},{2,0},{3,1},{4,6},{5,7},{6,4},{7,5},{8,10},{9,11},{10,... | collective-permute-start | bytes 884744 | tf_op jit(solution)/shard_map/ppermute | solution.py:279
  185.9 11.6 %collective-permute-start.3 = (f32[192,384]{1,0:T(8,128)S(1)}, f32[192,384]{1,0:T(8,128)S(1)}, u32[]{:S(2)}, u32[]{:S(2)}) collective-permute-start(f32[192,384]{1,0:T(8,128)S(1)} %bitcast.98), channel_id=1, source_target_pairs={{0,8},{1,9},{2,10},{3,11},{4,12},{5,13},{6,14},{7,15},{8,0},{9,1},... | collective-permute-start | bytes 884744 | tf_op jit(solution)/shard_map/ppermute | solution.py:279
  187.6 24.1 %copy-start.1 = (bf16[768,256]{1,0:T(8,128)(2,1)S(1)}, bf16[768,256]{1,0:T(8,128)(2,1)}, u32[]{:S(2)}) copy-start(bf16[768,256]{1,0:T(8,128)(2,1)} %param.32) | copy-start | bytes 1179652
  187.7 13.8 %collective-permute-start.8 = (f32[192,384]{1,0:T(8,128)S(1)}, f32[192,384]{1,0:T(8,128)S(1)}, u32[]{:S(2)}, u32[]{:S(2)}) collective-permute-start(f32[192,384]{1,0:T(8,128)S(1)} %bitcast.99), channel_id=1, source_target_pairs={{0,8},{1,9},{2,10},{3,11},{4,12},{5,13},{6,14},{7,15},{8,0},{9,1},... | collective-permute-start | bytes 884744 | tf_op jit(solution)/shard_map/ppermute | solution.py:279
  197.6 10.1 %collective-permute-start.4 = (f32[96,384]{1,0:T(8,128)S(1)}, f32[96,384]{1,0:T(8,128)S(1)}, u32[]{:S(2)}, u32[]{:S(2)}) collective-permute-start(f32[96,384]{1,0:T(8,128)S(1)} %dynamic-slice_bitcast_fusion.1), channel_id=1, source_target_pairs={{0,16},{1,17},{2,18},{3,19},{4,20},{5,21},{6,22},{7,23},{8,24},{9,... | collective-permute-start | bytes 442376 | tf_op jit(solution)/shard_map/ppermute | solution.py:279
  201.6 9.3 %collective-permute-start.9 = (f32[96,384]{1,0:T(8,128)S(1)}, f32[96,384]{1,0:T(8,128)S(1)}, u32[]{:S(2)}, u32[]{:S(2)}) collective-permute-start(f32[96,384]{1,0:T(8,128)S(1)} %dynamic-slice_bitcast_fusion), channel_id=1, source_target_pairs={{0,16},{1,17},{2,18},{3,19},{4,20},{5,21},{6,22},{7,23},{8,24},{9,... | collective-permute-start | bytes 442376 | tf_op jit(solution)/shard_map/ppermute | solution.py:279

commit v3 on v2

--- a/solution.py
+++ b/solution.py
@@ -270,7 +270,7 @@
             pltpu.VMEM((positions, tiles, LANES), jnp.float32),
         ],
         compiler_params=pltpu.CompilerParams(vmem_limit_bytes=VMEM_LIMIT),
-        cost_estimate=pl.CostEstimate(flops=40_000_000, bytes_accessed=8_000_000, transcendentals=0),
+        cost_estimate=pl.CostEstimate(flops=10_000_000_000, bytes_accessed=40_000_000, transcendentals=0),
     )(grad_normed, hat, rstd, x, vectors)
 
 
@@ -279,30 +279,28 @@
     return lax.ppermute(values, AXES, pairs)
 
 
-def halve_scatter(partial_sum, order, narrow, devices, index):
-    bits = devices.bit_length() - 1
-    rows, columns = partial_sum.shape
-    current = partial_sum.reshape((2,) * bits + (rows // devices, columns))
-    left = list(range(bits - 1, -1, -1))
-    for bit in order:
-        axis = left.index(bit)
-        left.pop(axis)
-        mine = (index >> bit) & 1
-        kept = lax.dynamic_index_in_dim(current, mine, axis, keepdims=False)
-        sent = lax.dynamic_index_in_dim(current, 1 - mine, axis, keepdims=False)
-        if bit in narrow:
-            sent = sent.astype(jnp.bfloat16)
-        shape = sent.shape
-        flat = sent.reshape(-1, columns)
-        current = kept + swap(flat, bit, devices).reshape(shape).astype(jnp.float32)
-    return current
+def halve_start(current, left, bit, narrow, devices, index):
+    columns = current.shape[-1]
+    axis = left.index(bit)
+    mine = (index >> bit) & 1
+    kept = lax.dynamic_index_in_dim(current, mine, axis, keepdims=False)
+    sent = lax.dynamic_index_in_dim(current, 1 - mine, axis, keepdims=False)
+    if bit in narrow:
+        sent = sent.astype(jnp.bfloat16)
+    arrived = swap(sent.reshape(-1, columns), bit, devices).reshape(sent.shape)
+    return kept + arrived.astype(jnp.float32), left[:axis] + left[axis + 1 :]
 
 
 def exchange_kernel(
     devices, n_slide, sums_ref, pooled_ref, grad_ref, head_ref,
     total_ref, all_pooled_ref, all_grad_ref, all_head_ref, landed, send_sem, recv_sem,
 ):
-    me = lax.axis_index("enc") * n_slide + lax.axis_index("slide")
+    n_enc = devices // n_slide
+    my_enc, my_slide = lax.axis_index("enc"), lax.axis_index("slide")
+    me = my_enc * n_slide + my_slide
+
+    def slot_of(device):
+        return lax.rem(device, n_slide) * n_enc + device // n_slide
 
     def place(device):
         return {"enc": device // n_slide, "slide": lax.rem(device, n_slide)}
@@ -329,37 +327,85 @@
     def sums(k, to, slot):
         return copy(0, k, sums_ref.at[to], landed.at[slot], to)
 
-    def others(k, to, slot):
+    def pooled(k, to, slot):
+        return copy(1, k, pooled_ref.at[to], all_pooled_ref.at[slot], to)
+
+    def spread(k, to, slot):
+        device = to * n_slide + my_slide
         return (
-            copy(1, k, pooled_ref.at[to], all_pooled_ref.at[slot], to),
-            copy(2, k, grad_ref, all_grad_ref.at[slot], to),
-            copy(3, k, head_ref, all_head_ref.at[slot], to),
+            copy(2, k, grad_ref, all_grad_ref.at[my_slide, slot], device),
+            copy(3, k, head_ref, all_head_ref.at[my_slide, slot], device),
         )
+
+    def each_enc(body):
+        def step(k, carry):
+            body(k, lax.rem(my_enc + k, n_enc), lax.rem(my_enc + n_enc - k, n_enc))
+            return carry
+
+        lax.fori_loop(1, n_enc, step, 0)
+
+    def flip(value, bit):
+        return value + (1 << bit) * (1 - 2 * lax.rem(value // (1 << bit), 2))
+
+    def passed(bit, held, first, receive):
+        peer = flip(my_slide, bit)
+        items = []
+        for q, mask in enumerate(held):
+            slot = peer if receive else my_slide
+            for m in mask:
+                slot = flip(slot, m)
+            for kind, ref in ((2, all_grad_ref), (3, all_head_ref)):
+                items.append(copy(
+                    kind, n_enc + first + q, ref.at[slot], ref.at[slot],
+                    my_enc * n_slide + peer))
+        return items
 
     def totals(k, to, slot):
         return copy(4, k, total_ref.at[me], total_ref.at[slot], to)
 
     each(lambda k, to, source: sums(k, to, me).start())
     landed[me] = sums_ref[me]
-    all_pooled_ref[me] = pooled_ref[me]
-    all_grad_ref[me] = grad_ref[...]
-    all_head_ref[me] = head_ref[...]
-
-    def start_others(k, to, source):
-        for item in others(k, to, me):
+    all_pooled_ref[slot_of(me)] = pooled_ref[me]
+    all_grad_ref[my_slide, my_enc] = grad_ref[...]
+    all_head_ref[my_slide, my_enc] = head_ref[...]
+
+    def start_spread(k, to, source):
+        for item in spread(k, to, my_enc):
             item.start()
 
-    each(start_others)
+    def wait_spread(k, to, source):
+        for item in spread(k, to, source):
+            item.wait_recv()
+
+    def sent_spread(k, to, source):
+        for item in spread(k, to, my_enc):
+            item.wait_send()
+
+    each_enc(start_spread)
+    each(lambda k, to, source: pooled(k, to, slot_of(me)).start())
     each(lambda k, to, source: sums(k, to, source).wait_recv())
     total_ref[me] = jnp.sum(landed[...], axis=0)
     each(lambda k, to, source: totals(k, to, me).start())
+    each_enc(wait_spread)
+    held, first = [()], 0
+    sent = []
+    for bit in range(n_slide.bit_length() - 2, -1, -1):
+        outgoing = passed(bit, held, first, False)
+        for item in outgoing:
+            item.start()
+        sent += outgoing
+        for item in passed(bit, held, first, True):
+            item.wait_recv()
+        first += len(held)
+        held = held + [mask + (bit,) for mask in held]
+    for item in sent:
+        item.wait_send()
+    each_enc(sent_spread)
 
     def finish(k, to, source):
         sums(k, to, me).wait_send()
-        for item in others(k, to, source):
-            item.wait_recv()
-        for item in others(k, to, me):
-            item.wait_send()
+        pooled(k, to, slot_of(source)).wait_recv()
+        pooled(k, to, slot_of(me)).wait_send()
         totals(k, to, source).wait_recv()
         totals(k, to, me).wait_send()
 
@@ -372,8 +418,8 @@
         out_shape=(
             jax.ShapeDtypeStruct(sums.shape, sums.dtype),
             jax.ShapeDtypeStruct(pooled.shape, pooled.dtype),
-            jax.ShapeDtypeStruct((devices,) + grad.shape, grad.dtype),
-            jax.ShapeDtypeStruct((devices,) + head.shape, head.dtype),
+            jax.ShapeDtypeStruct((n_slide, devices // n_slide) + grad.shape, grad.dtype),
+            jax.ShapeDtypeStruct((n_slide, devices // n_slide) + head.shape, head.dtype),
         ),
         in_specs=whole_vmem(4),
         out_specs=tuple(whole_vmem(4)),
@@ -464,12 +510,27 @@
     xs = list(range(1, inner))
     rest = list(range(inner, bits))
     narrow = (1, inner)
-    first = halve_scatter(first, [0] + xs + rest, narrow, devices, index)
-    second = halve_scatter(second, [0] + rest[:1] + xs + rest[1:], narrow, devices, index)
-    grad_w_in = jnp.concatenate([first, second], axis=1)
-
+    orders = ([0] + xs + rest, [0] + rest[:1] + xs + rest[1:])
+    current = [
+        part.reshape((2,) * bits + (ff // devices, channels // 2)) for part in (first, second)
+    ]
+    left = [list(range(bits - 1, -1, -1))] * 2
+
+    def stage(number):
+        for part in range(2):
+            current[part], left[part] = halve_start(
+                current[part], left[part], orders[part][number], narrow, devices, index
+            )
+
+    stage(0)
     grad_normed = jnp.dot(grad_hidden, w_in, preferred_element_type=f32)
+    grad_normed, current[0], current[1] = lax.optimization_barrier(
+        (grad_normed, current[0], current[1])
+    )
+    stage(1)
     small = prepare_back(grad_normed, hat, rstd, x, vectors)
+    small, current[0], current[1] = lax.optimization_barrier((small, current[0], current[1]))
+    stage(2)
     bundle = jnp.concatenate(
         [
             small, grad_out_bias[None], grad_scale[None], grad_fgain[None], grad_fbias[None],
@@ -486,6 +547,10 @@
     bundle, mine, all_grad, head_parts = exchange(
         devices, n_slide, bundle, mine, grad_projected, head_rows
     )
+    bundle, current[0], current[1] = lax.optimization_barrier((bundle, current[0], current[1]))
+    for number in range(3, bits):
+        stage(number)
+    grad_w_in = jnp.concatenate(current, axis=1)
     bundle = bundle.reshape(-1, channels)
     head_parts = head_parts.reshape(-1, channels + genes)
     grad_head_w = lax.dot_general(

time: 212 us -> 186 us (0.88)
  Pallas kernels: 110 us -> 93.8 us
  waiting for transfers between devices: 38.1 us -> 22.2 us
  other arithmetic: 10.1 us -> 14.2 us
    pallas_call x1, Pallas kernels: 49.1 us -> 32.7 us  [exchange(): pl.pallas_call(partial(exchange_kernel, devices, n_slide), out_shape=(jax...]
    ppermute x10, waiting for transfers between devices: 38.1 us -> 22.2 us  [swap(): return lax.ppermute(values, AXES, pairs)]
    add x9 -> x10, other arithmetic: 4.92 us -> 8 us  [halve_start(): return (kept + arrived.astype(jnp.float32), left[:axis] + left[axis + 1:])]
  transfers between devices with their start and end apart: 10 -> 10, of which waited for: 8 -> 4; matrix products, arithmetic and copies ran while one was open for 12% -> 15% of each run, Pallas kernels for 31% -> 9%
where the time goes in v3:
time: 186 us; the launch traced here: 185 us
  Pallas kernels  93.8 us (50%)
  waiting for transfers between devices  22.2 us (12%)
  matrix products  20.1 us (11%)
  local copies, waits for them, and re-layouts  16.4 us (9%)
  other arithmetic  14.2 us (8%)
  starting transfers between devices  10.2 us (5%)
  blocking collectives  7.02 us (4%)
    pallas_call x1, Pallas kernels, exchange(): pl.pallas_call(partial(exchange_kernel, devices, n_slide), out_shape=(jax...  32.7 us
    ppermute x10, waiting for transfers between devices, swap(): return lax.ppermute(values, AXES, pairs)  22.2 us
    pallas_call x1, Pallas kernels, prepare(): pl.pallas_call(prepare_kernel, out_shape=(jax.ShapeDtypeStruct((rows, cha...  17.6 us
    pallas_call x1, Pallas kernels, prepare_back(): pl.pallas_call(prepare_back_kernel, out_shape=jax.ShapeDtypeStruct((posit...  15.9 us
    pallas_call x1, Pallas kernels, hidden_layer(): pl.pallas_call(hidden_kernel, grid=(ff // width,), out_shape=(jax.ShapeDt...  14.1 us
    pallas_call x1, Pallas kernels, grad_hidden_layer(): pl.pallas_call(grad_hidden_kernel, grid=(ff // width,), out_shape=(jax.Sh...  13.5 us
    ppermute x10, starting transfers between devices, swap(): return lax.ppermute(values, AXES, pairs)  10.2 us
    dot_general x1, matrix products, per_device(): grad_normed = jnp.dot(grad_hidden, w_in, preferred_element_type=f32)  9.27 us
  transfers between devices with their start and end apart: 10, of which 4 were waited for; matrix products, arithmetic and copies ran while one was open for 15% of the time, Pallas kernels for 9%

profile of v3, /device:TPU:0, one launch (start us, length us, event | category | flops | bytes accessed | tf_op | source)
XLA Modules:
  0.0 185.2 jit_solution(14485606568468793599)
XLA Ops:
  0.6 0.7 stack.12
  1.4 0.7 stack.13
  2.1 0.7 stack.14
  2.8 1.3 broadcast_in_dim.12.bias_ref
  4.1 0.6 maximum_convert_fusion.vec_ref
  4.7 17.6 %shard_map.224 = (bf16[784,768]{1,0:T(8,128)(2,1)}, f32[784,768]{1,0:T(8,128)}, f32[784,128]{1,0:T(8,128)}, f32[16,768]{1,0:T(8,128)}) custom-call(bf16[49,16,768]{2,1,0:T(8,128)(2,1)} %bitcast.89, bf16[49,768]{1,0:T(8,128)(2,1)} %k_ref.1, f32[3,768]{1,0:T(4,128)} %maximum_convert_fusion.vec_ref), custom_call_target="tpu_custom_call" | custom-call | flops 40000000 | bytes 5000000 | tf_op jit(solution)/shard_map/pallas_call | solution.py:84
  22.3 14.1 %shard_map.225 = (f32[16,3072]{1,0:T(8,128)}, f32[784,3072]{1,0:T(8,128)}) custom-call(bf16[784,768]{1,0:T(8,128)(2,1)} %get-tuple-element.31.normed_ref, bf16[3072,768]{1,0:T(8,128)(2,1)} %w_ref.1, bf16[1,3072]{1,0:T(2,128)(2,1)} %broadcast_in_dim.12.bias_ref), custom_call_target="tpu_custom_call" | custom-call | flops 3699376128 | bytes 20000000 | tf_op jit(solution)/shard_map/pallas_call | solution.py:132
  36.4 0.9 reduce-precision_convert_fusion.1
  37.5 0.9 fusion.6
  39.2 7.0 %all-gather.1 = f32[4,9,768]{2,1,0:T(8,128)S(1)} all-gather(f32[1,9,768]{2,1,0:T(8,128)S(1)} %maximum_bitcast_fusion), channel_id=2, replica_groups=mesh['enc'=8,'slide'=4] {'slide'}, dimensions={0}, use_global_device_ids=true | all-gather | bytes 138240 | tf_op jit(solution)/shard_map/all_gather | solution.py:478
  48.0 4.4 %fusion.28.ga_ref = f32[16,3072]{1,0:T(8,128)} fusion(bf16[16,768]{1,0:T(8,128)(2,1)S(1)} %get-tuple-element.67.grad_ref, bf16[3072,768]{1,0:T(8,128)(2,1)} %param.27), kind=kOutput, calls=%fused_computation.89 | convolution fusion | flops 75497472 | bytes 4939776 | tf_op jit(solution)/shard_map/dot_general | solution.py:503
  52.4 13.5 %shard_map.226 = (bf16[784,3072]{1,0:T(8,128)(2,1)}, f32[3072,384]{1,0:T(8,128)}, f32[3072,384]{1,0:T(8,128)}, f32[1,3072]{1,0:T(1,128)}) custom-call(f32[784,3072]{1,0:T(8,128)} %get-tuple-element.32.slope_ref, f32[16,3072]{1,0:T(8,128)} %fusion.28.ga_ref, bf16[784,768]{1,0:T(8,128)(2,1)} %get-tuple-element.31.normed_ref), custom_call_target="tpu_custom_call" | custom-call | flops 3699376128 | bytes 25000000 | tf_op jit(solution)/shard_map/pallas_call | solution.py:186
  65.9 3.4 %constant_dynamic-slice_fusion.2 = f32[2,2,2,2,1,96,384]{6,5,4,3,2,1,0:T(8,128)} fusion(f32[2,2,2,2,2,96,384]{6,5,4,3,2,1,0:T(8,128)} %bitcast.83, s32[]{:T(128)S(6)} %select_n.51), kind=kLoop, calls=%fused_computation.67 | loop fusion | bytes 4718596 | tf_op jit(solution)/shard_map/jit(dynamic_index_in_dim)/dynamic_slice | solution.py:287
  69.7 1.6 constant_dynamic-slice_fusion.3
  72.1 0.7 reduce.3
  72.9 0.9 copy.37
  73.7 0.6 dynamic-slice_bitcast_fusion.2
  74.3 0.6 fusion.18.head_ref
  74.9 9.3 %fusion.29.gn_ref = f32[784,768]{1,0:T(8,128)} fusion(bf16[784,3072]{1,0:T(8,128)(2,1)} %get-tuple-element.35, bf16[3072,768]{1,0:T(8,128)(2,1)} %w_ref.1), kind=kOutput, calls=%fused_computation.90 | convolution fusion | flops 3699376128 | bytes 11943936 | tf_op jit(solution)/shard_map/dot_general | solution.py:526
  84.2 1.9 %bitcast_add_fusion = f32[2,2,2,2,96,384]{5,4,3,2,1,0:T(8,128)S(1)} fusion(f32[2,2,2,2,96,384]{5,4,3,2,1,0:T(8,128)} %bitcast.12, f32[2,2,2,2,2,96,384]{6,5,4,3,2,1,0:T(8,128)S(1)} %bitcast.86, s32[]{:T(128)S(6)} %select_n.50), kind=kLoop, calls=%fused_computation | loop fusion | flops 589824 | bytes 7077892 | tf_op jit(solution)/shard_map/add | solution.py:291
  86.1 2.6 %bitcast_add_fusion.1 = f32[2,2,2,2,96,384]{5,4,3,2,1,0:T(8,128)S(1)} fusion(f32[2,2,2,2,96,384]{5,4,3,2,1,0:T(8,128)} %bitcast.8, f32[2,2,2,2,2,96,384]{6,5,4,3,2,1,0:T(8,128)} %bitcast.81, s32[]{:T(128)S(6)} %select_n.50), kind=kLoop, calls=%fused_computation.1 | loop fusion | flops 589824 | bytes 7077892 | tf_op jit(solution)/shard_map/add | solution.py:291
  88.8 1.8 collective-permute-start.3
  90.7 1.6 collective-permute-start.2
  92.3 15.9 %shard_map.227 = f32[52,768]{1,0:T(8,128)} custom-call(f32[784,768]{1,0:T(8,128)} %fusion.29.gn_ref, f32[784,768]{1,0:T(8,128)} %get-tuple-element.39.hat_ref, f32[784,128]{1,0:T(8,128)} %get-tuple-element.40.rstd_ref, bf16[49,16,768]{2,1,0:T(8,128)(2,1)} %bitcast.90, f32[3,768]{1,0:T(4,128)} %maximum_convert_fusion.vec_ref), custom_call_target="tpu_custom_call" | custom-call | flops 10000000000 | bytes 40000000 | tf_op jit(solution)/shard_map/pallas_call | solution.py:263
  108.1 1.2 convert_add_fusion
  109.6 0.8 reshape.171.sums_ref
  110.4 32.7 %shard_map.228 = (f32[32,2,768]{2,1,0:T(2,128)}, f32[32,16,96]{2,1,0:T(8,128)}, bf16[4,8,16,768]{3,2,1,0:T(8,128)(2,1)}, f32[4,8,2,1024]{3,2,1,0:T(2,128)}) custom-call(f32[32,2,768]{2,1,0:T(2,128)} %reshape.171.sums_ref, f32[32,16,96]{2,1,0:T(8,128)} %bitcast.91, bf16[16,768]{1,0:T(8,128)(2,1)} %copy-done.7, f32[2,1024]{1,0:T(2,128)} %fusion.18.head_ref), custom_call_target="tpu_custom_call" | custom-call | flops 1000000 | bytes 40000000 | tf_op jit(solution)/shard_map/pallas_call | solution.py:416
  143.1 1.1 fusion.2
  144.2 0.7 collective-permute-start.5
  145.0 0.7 dynamic-slice_convert_fusion.3
  145.7 1.4 collective-permute-start.4
  147.1 1.4 fusion.30
  148.6 1.0 convolution_add_fusion
  149.6 1.1 reshape.180
  150.7 2.9 %collective-permute-done.5 = bf16[384,384]{1,0:T(8,128)(2,1)S(1)} collective-permute-done((bf16[384,384]{1,0:T(8,128)(2,1)S(1)}, bf16[384,384]{1,0:T(8,128)(2,1)S(1)}, u32[]{:S(2)}, u32[]{:S(2)}) %collective-permute-start.5) | collective-permute-done | bytes 294944 | tf_op jit(solution)/shard_map/ppermute | solution.py:279
  153.6 0.7 copy-done.5
  154.3 1.0 convert_add_fusion.2
  155.4 1.0 convert_add_fusion.3
  156.4 3.9 %collective-permute-start.6 = (f32[192,384]{1,0:T(8,128)S(1)}, f32[192,384]{1,0:T(8,128)S(1)}, u32[]{:S(2)}, u32[]{:S(2)}) collective-permute-start(f32[192,384]{1,0:T(8,128)S(1)} %bitcast.99), channel_id=1, source_target_pairs={{0,8},{1,9},{2,10},{3,11},{4,12},{5,13},{6,14},{7,15},{8,0},{9,1},... | collective-permute-start | bytes 884744 | tf_op jit(solution)/shard_map/ppermute | solution.py:279
  160.4 1.7 fusion.4
  162.1 0.6 slice_reduce_fusion.1
  162.8 0.7 slice.52
  163.5 0.6 slice.53
  164.2 0.6 reshape.179
  164.8 3.4 %collective-permute-done.6 = f32[192,384]{1,0:T(8,128)S(1)} collective-permute-done((f32[192,384]{1,0:T(8,128)S(1)}, f32[192,384]{1,0:T(8,128)S(1)}, u32[]{:S(2)}, u32[]{:S(2)}) %collective-permute-start.6) | collective-permute-done | bytes 294944 | tf_op jit(solution)/shard_map/ppermute | solution.py:279
  168.4 8.4 %collective-permute-done.8 = f32[192,384]{1,0:T(8,128)S(1)} collective-permute-done((f32[192,384]{1,0:T(8,128)S(1)}, f32[192,384]{1,0:T(8,128)S(1)}, u32[]{:S(2)}, u32[]{:S(2)}) %collective-permute-start.8) | collective-permute-done | bytes 294944 | tf_op jit(solution)/shard_map/ppermute | solution.py:279
  176.9 7.5 %collective-permute-done.9 = f32[96,384]{1,0:T(8,128)S(1)} collective-permute-done((f32[96,384]{1,0:T(8,128)S(1)}, f32[96,384]{1,0:T(8,128)S(1)}, u32[]{:S(2)}, u32[]{:S(2)}) %collective-permute-start.9) | collective-permute-done | bytes 147488 | tf_op jit(solution)/shard_map/ppermute | solution.py:279
  184.4 0.7 pad_maximum_fusion
  (112 shorter events, 4.7 us)
Async XLA Ops:
  0.6 45.8 %copy-start = (bf16[768,256]{1,0:T(8,128)(2,1)S(1)}, bf16[768,256]{1,0:T(8,128)(2,1)}, u32[]{:S(2)}) copy-start(bf16[768,256]{1,0:T(8,128)(2,1)} %param.32) | copy-start | bytes 1179652
  4.7 32.8 %slice-start = ((s8[4718592]{0:T(1024)(128)(4,1)}), s8[4194304]{0:T(1024)(128)(4,1)S(1)}, s32[]{:S(2)}) async-start(s8[4718592]{0:T(1024)(128)(4,1)} %bitcast.79), calls=%async_computation | async-start | bytes 8388608
  22.3 15.1 %copy-start.11 = (bf16[768]{0:T(1024)(128)(2,1)S(1)}, bf16[768]{0:T(1024)(128)(2,1)}, u32[]{:S(2)}) copy-start(bf16[768]{0:T(1024)(128)(2,1)} %param.29) | copy-start | bytes 4612
  22.3 15.1 %copy-start.12 = (bf16[768]{0:T(1024)(128)(2,1)S(1)}, bf16[768]{0:T(1024)(128)(2,1)}, u32[]{:S(2)}) copy-start(bf16[768]{0:T(1024)(128)(2,1)} %param.28) | copy-start | bytes 4612
  22.3 15.1 %slice-start.1 = ((s8[4718592]{0:T(1024)(128)(4,1)}), s8[524288]{0:T(1024)(128)(4,1)S(1)}, s32[]{:S(2)}) async-start(s8[4718592]{0:T(1024)(128)(4,1)} %bitcast.79), calls=%async_computation.1 | async-start | bytes 1048576
  37.5 0.9 copy-start.9
  37.5 1.3 copy-start.13
  37.5 1.3 copy-start.14
  37.5 1.3 copy-start.15
  37.5 1.3 copy-start.17
  37.5 1.3 copy-start.18
  37.5 8.8 %copy-start.16 = (bf16[256]{0:T(256)(128)(2,1)S(1)}, bf16[256]{0:T(256)(128)(2,1)}, u32[]{:S(2)}) copy-start(bf16[256]{0:T(256)(128)(2,1)} %param.33) | copy-start | bytes 1540
  48.0 4.4 %copy-start.7 = (bf16[16,768]{1,0:T(8,128)(2,1)}, bf16[16,768]{1,0:T(8,128)(2,1)S(1)}, u32[]{:S(2)}) copy-start(bf16[16,768]{1,0:T(8,128)(2,1)S(1)} %get-tuple-element.67.grad_ref) | copy-start | bytes 73732
  65.9 3.8 %copy-start.2 = (f32[3072,384]{1,0:T(8,128)S(1)}, f32[3072,384]{1,0:T(8,128)}, u32[]{:S(2)}) copy-start(f32[3072,384]{1,0:T(8,128)} %get-tuple-element.36) | copy-start | bytes 14155780
  69.3 14.9 %collective-permute-start.1 = (f32[1536,384]{1,0:T(8,128)}, f32[1536,384]{1,0:T(8,128)}, u32[]{:S(2)}, u32[]{:S(2)}) collective-permute-start(f32[1536,384]{1,0:T(8,128)} %bitcast.11), channel_id=1, source_target_pairs={{0,1},{1,0},{2,3},{3,2},{4,5},{5,4},{6,7},{7,6},{8,9},{9,8},{10,11... | collective-permute-start | bytes 7077896 | tf_op jit(solution)/shard_map/ppermute | solution.py:279
  69.7 1.8 copy-start.4
  69.7 2.5 %copy-start.10 = (f32[1,3072]{1,0:T(1,128)S(1)}, f32[1,3072]{1,0:T(1,128)}, u32[]{:S(2)}) copy-start(f32[1,3072]{1,0:T(1,128)} %get-tuple-element.44) | copy-start | bytes 36868
  71.3 14.8 %collective-permute-start = (f32[1536,384]{1,0:T(8,128)}, f32[1536,384]{1,0:T(8,128)}, u32[]{:S(2)}, u32[]{:S(2)}) collective-permute-start(f32[1536,384]{1,0:T(8,128)} %bitcast.7), channel_id=1, source_target_pairs={{0,1},{1,0},{2,3},{3,2},{4,5},{5,4},{6,7},{7,6},{8,9},{9,8},{10,11... | collective-permute-start | bytes 7077896 | tf_op jit(solution)/shard_map/ppermute | solution.py:279
  72.9 11.3 %slice-start.2 = ((s8[4718592]{0:T(1024)(128)(4,1)}), s8[524288]{0:T(1024)(128)(4,1)S(1)}, s32[]{:S(2)}) async-start(s8[4718592]{0:T(1024)(128)(4,1)} %bitcast.84), calls=%async_computation.2 | async-start | bytes 1048576
  74.9 9.3 %slice-start.3 = ((s8[4718592]{0:T(1024)(128)(4,1)}), s8[4194304]{0:T(1024)(128)(4,1)S(1)}, s32[]{:S(2)}) async-start(s8[4718592]{0:T(1024)(128)(4,1)} %bitcast.84), calls=%async_computation.3 | async-start | bytes 8388608
  88.8 19.3 %collective-permute-start.3 = (bf16[768,384]{1,0:T(8,128)(2,1)S(1)}, bf16[768,384]{1,0:T(8,128)(2,1)}, u32[]{:S(2)}, u32[]{:S(2)}) collective-permute-start(bf16[768,384]{1,0:T(8,128)(2,1)S(1)} %bitcast.93), channel_id=1, source_target_pairs={{0,4},{1,5},{2,6},{3,7},{4,0},{5,1},{6,2},{7,3},{8,12},{9,13},{10,... | collective-permute-start | bytes 1769480 | tf_op jit(solution)/shard_map/ppermute | solution.py:279
  90.7 18.6 %collective-permute-start.2 = (bf16[768,384]{1,0:T(8,128)(2,1)S(1)}, bf16[768,384]{1,0:T(8,128)(2,1)S(1)}, u32[]{:S(2)}, u32[]{:S(2)}) collective-permute-start(bf16[768,384]{1,0:T(8,128)(2,1)S(1)} %bitcast.92), channel_id=1, source_target_pairs={{0,2},{1,3},{2,0},{3,1},{4,6},{5,7},{6,4},{7,5},{8,10},{9,11},{10,... | collective-permute-start | bytes 1769480 | tf_op jit(solution)/shard_map/ppermute | solution.py:279
  108.1 1.3 copy-start.8
  143.1 5.5 %copy-start.3 = (bf16[4,8,16,768]{3,2,1,0:T(8,128)(2,1)S(1)}, bf16[4,8,16,768]{3,2,1,0:T(8,128)(2,1)}, u32[]{:S(2)}) copy-start(bf16[4,8,16,768]{3,2,1,0:T(8,128)(2,1)} %get-tuple-element.51) | copy-start | bytes 2359300
  144.2 9.4 %collective-permute-start.5 = (bf16[384,384]{1,0:T(8,128)(2,1)S(1)}, bf16[384,384]{1,0:T(8,128)(2,1)S(1)}, u32[]{:S(2)}, u32[]{:S(2)}) collective-permute-start(bf16[384,384]{1,0:T(8,128)(2,1)S(1)} %bitcast.100), channel_id=1, source_target_pairs={{0,2},{1,3},{2,0},{3,1},{4,6},{5,7},{6,4},{7,5},{8,10},{9,11},{10,... | collective-permute-start | bytes 884744 | tf_op jit(solution)/shard_map/ppermute | solution.py:279
  145.7 9.7 %collective-permute-start.4 = (bf16[384,384]{1,0:T(8,128)(2,1)}, bf16[384,384]{1,0:T(8,128)(2,1)}, u32[]{:S(2)}, u32[]{:S(2)}) collective-permute-start(bf16[384,384]{1,0:T(8,128)(2,1)} %bitcast.21), channel_id=1, source_target_pairs={{0,4},{1,5},{2,6},{3,7},{4,0},{5,1},{6,2},{7,3},{8,12},{9,13},{10,... | collective-permute-start | bytes 884744 | tf_op jit(solution)/shard_map/ppermute | solution.py:279
  150.7 12.0 %copy-start.6 = (f32[32,2,768]{2,1,0:T(2,128)S(1)}, f32[32,2,768]{2,1,0:T(2,128)}, u32[]{:S(2)}) copy-start(f32[32,2,768]{2,1,0:T(2,128)} %get-tuple-element.52) | copy-start | bytes 589828
  153.6 0.7 copy-start.5
  156.4 11.8 %collective-permute-start.6 = (f32[192,384]{1,0:T(8,128)S(1)}, f32[192,384]{1,0:T(8,128)S(1)}, u32[]{:S(2)}, u32[]{:S(2)}) collective-permute-start(f32[192,384]{1,0:T(8,128)S(1)} %bitcast.99), channel_id=1, source_target_pairs={{0,8},{1,9},{2,10},{3,11},{4,12},{5,13},{6,14},{7,15},{8,0},{9,1},... | collective-permute-start | bytes 884744 | tf_op jit(solution)/shard_map/ppermute | solution.py:279
  162.7 22.5 %copy-start.1 = (bf16[768,256]{1,0:T(8,128)(2,1)S(1)}, bf16[768,256]{1,0:T(8,128)(2,1)}, u32[]{:S(2)}) copy-start(bf16[768,256]{1,0:T(8,128)(2,1)} %param.32) | copy-start | bytes 1179652
  164.1 12.6 %collective-permute-start.8 = (f32[192,384]{1,0:T(8,128)S(1)}, f32[192,384]{1,0:T(8,128)S(1)}, u32[]{:S(2)}, u32[]{:S(2)}) collective-permute-start(f32[192,384]{1,0:T(8,128)S(1)} %bitcast.101), channel_id=1, source_target_pairs={{0,8},{1,9},{2,10},{3,11},{4,12},{5,13},{6,14},{7,15},{8,0},{9,1},... | collective-permute-start | bytes 884744 | tf_op jit(solution)/shard_map/ppermute | solution.py:279
  168.3 8.6 %collective-permute-start.7 = (f32[96,384]{1,0:T(8,128)S(1)}, f32[96,384]{1,0:T(8,128)S(1)}, u32[]{:S(2)}, u32[]{:S(2)}) collective-permute-start(f32[96,384]{1,0:T(8,128)S(1)} %dynamic-slice_bitcast_fusion.1), channel_id=1, source_target_pairs={{0,16},{1,17},{2,18},{3,19},{4,20},{5,21},{6,22},{7,23},{8,24},{9,... | collective-permute-start | bytes 442376 | tf_op jit(solution)/shard_map/ppermute | solution.py:279
  176.8 7.6 %collective-permute-start.9 = (f32[96,384]{1,0:T(8,128)S(1)}, f32[96,384]{1,0:T(8,128)S(1)}, u32[]{:S(2)}, u32[]{:S(2)}) collective-permute-start(f32[96,384]{1,0:T(8,128)S(1)} %dynamic-slice_bitcast_fusion), channel_id=1, source_target_pairs={{0,16},{1,17},{2,18},{3,19},{4,20},{5,21},{6,22},{7,23},{8,24},{9,... | collective-permute-start | bytes 442376 | tf_op jit(solution)/shard_map/ppermute | solution.py:279

commit v4 on v3

--- a/solution.py
+++ b/solution.py
@@ -432,7 +432,7 @@
             collective_id=0, has_side_effects=True, vmem_limit_bytes=VMEM_LIMIT
         ),
         cost_estimate=pl.CostEstimate(
-            flops=1_000_000, bytes_accessed=40_000_000, transcendentals=0
+            flops=10_000_000_000, bytes_accessed=80_000_000, transcendentals=0
         ),
     )(sums, pooled, grad, head)
 
@@ -509,7 +509,7 @@
     inner = n_slide.bit_length() - 1
     xs = list(range(1, inner))
     rest = list(range(inner, bits))
-    narrow = (1, inner)
+    narrow = (1, inner, inner + 1)
     orders = ([0] + xs + rest, [0] + rest[:1] + xs + rest[1:])
     current = [
         part.reshape((2,) * bits + (ff // devices, channels // 2)) for part in (first, second)
@@ -547,7 +547,9 @@
     bundle, mine, all_grad, head_parts = exchange(
         devices, n_slide, bundle, mine, grad_projected, head_rows
     )
-    bundle, current[0], current[1] = lax.optimization_barrier((bundle, current[0], current[1]))
+    bundle, mine, all_grad, head_parts, current[0], current[1] = lax.optimization_barrier(
+        (bundle, mine, all_grad, head_parts, current[0], current[1])
+    )
     for number in range(3, bits):
         stage(number)
     grad_w_in = jnp.concatenate(current, axis=1)

time: 186 us -> 177 us (0.952)
  waiting for transfers between devices: 22.2 us -> 16.2 us
    ppermute x10, waiting for transfers between devices: 22.2 us -> 16.2 us  [swap(): return lax.ppermute(values, AXES, pairs)]
    dynamic_slice x4 -> x2, local copies, waits for them, and re-layouts: 5.07 us -> 5.01 us  [halve_start(): sent = lax.dynamic_index_in_dim(current, 1 - mine, axis, keepdims=False)]
  transfers between devices with their start and end apart: 10 -> 10, of which waited for: 4 -> 3; matrix products, arithmetic and copies ran while one was open for 15% -> 15% of each run, Pallas kernels for 9% -> 28%
where the time goes in v4:
time: 177 us; the launch traced here: 176 us
  Pallas kernels  94.1 us (53%)
  matrix products  18.9 us (11%)
  waiting for transfers between devices  16.2 us (9%)
  local copies, waits for them, and re-layouts  16.1 us (9%)
  other arithmetic  14 us (8%)
  starting transfers between devices  8.56 us (5%)
  blocking collectives  7.02 us (4%)
    pallas_call x1, Pallas kernels, exchange(): pl.pallas_call(partial(exchange_kernel, devices, n_slide), out_shape=(jax...  33.2 us
    pallas_call x1, Pallas kernels, prepare(): pl.pallas_call(prepare_kernel, out_shape=(jax.ShapeDtypeStruct((rows, cha...  17.6 us
    ppermute x10, waiting for transfers between devices, swap(): return lax.ppermute(values, AXES, pairs)  16.2 us
    pallas_call x1, Pallas kernels, prepare_back(): pl.pallas_call(prepare_back_kernel, out_shape=jax.ShapeDtypeStruct((posit...  15.8 us
    pallas_call x1, Pallas kernels, hidden_layer(): pl.pallas_call(hidden_kernel, grid=(ff // width,), out_shape=(jax.ShapeDt...  14 us
    pallas_call x1, Pallas kernels, grad_hidden_layer(): pl.pallas_call(grad_hidden_kernel, grid=(ff // width,), out_shape=(jax.Sh...  13.5 us
    dot_general x1, matrix products, per_device(): grad_normed = jnp.dot(grad_hidden, w_in, preferred_element_type=f32)  9.23 us
    add x10, other arithmetic, halve_start(): return (kept + arrived.astype(jnp.float32), left[:axis] + left[axis + 1:])  8.83 us
  transfers between devices with their start and end apart: 10, of which 3 were waited for; matrix products, arithmetic and copies ran while one was open for 15% of the time, Pallas kernels for 28%

profile of v4, /device:TPU:0, one launch (start us, length us, event | category | flops | bytes accessed | tf_op | source)
XLA Modules:
  0.0 176.2 jit_solution(428530341810810484)
XLA Ops:
  0.6 0.7 stack.12
  1.4 0.7 stack.13
  2.1 0.7 stack.14
  2.8 1.3 broadcast_in_dim.12.bias_ref
  4.1 0.6 maximum_convert_fusion.vec_ref
  4.7 17.6 %shard_map.224 = (bf16[784,768]{1,0:T(8,128)(2,1)}, f32[784,768]{1,0:T(8,128)}, f32[784,128]{1,0:T(8,128)}, f32[16,768]{1,0:T(8,128)}) custom-call(bf16[49,16,768]{2,1,0:T(8,128)(2,1)} %bitcast.91, bf16[49,768]{1,0:T(8,128)(2,1)} %k_ref.1, f32[3,768]{1,0:T(4,128)} %maximum_convert_fusion.vec_ref), custom_call_target="tpu_custom_call" | custom-call | flops 40000000 | bytes 5000000 | tf_op jit(solution)/shard_map/pallas_call | solution.py:84
  22.3 14.0 %shard_map.225 = (f32[16,3072]{1,0:T(8,128)}, f32[784,3072]{1,0:T(8,128)}) custom-call(bf16[784,768]{1,0:T(8,128)(2,1)} %get-tuple-element.34.normed_ref, bf16[3072,768]{1,0:T(8,128)(2,1)} %w_ref.1, bf16[1,3072]{1,0:T(2,128)(2,1)} %broadcast_in_dim.12.bias_ref), custom_call_target="tpu_custom_call" | custom-call | flops 3699376128 | bytes 20000000 | tf_op jit(solution)/shard_map/pallas_call | solution.py:132
  36.4 0.9 reduce-precision_convert_fusion.1
  37.5 0.9 fusion.6
  39.2 7.0 %all-gather.1 = f32[4,9,768]{2,1,0:T(8,128)S(1)} all-gather(f32[1,9,768]{2,1,0:T(8,128)S(1)} %maximum_bitcast_fusion), channel_id=2, replica_groups=mesh['enc'=8,'slide'=4] {'slide'}, dimensions={0}, use_global_device_ids=true | all-gather | bytes 138240 | tf_op jit(solution)/shard_map/all_gather | solution.py:478
  46.4 0.4 multiply_reduce_fusion.5
  46.8 0.4 fusion
  47.2 0.4 multiply_reduce_fusion
  48.0 4.4 %fusion.28.ga_ref = f32[16,3072]{1,0:T(8,128)} fusion(bf16[16,768]{1,0:T(8,128)(2,1)S(1)} %get-tuple-element.73.grad_ref, bf16[3072,768]{1,0:T(8,128)(2,1)} %param.27), kind=kOutput, calls=%fused_computation.89 | convolution fusion | flops 75497472 | bytes 4939776 | tf_op jit(solution)/shard_map/dot_general | solution.py:503
  52.3 13.5 %shard_map.226 = (bf16[784,3072]{1,0:T(8,128)(2,1)}, f32[3072,384]{1,0:T(8,128)}, f32[3072,384]{1,0:T(8,128)}, f32[1,3072]{1,0:T(1,128)}) custom-call(f32[784,3072]{1,0:T(8,128)} %get-tuple-element.35.slope_ref, f32[16,3072]{1,0:T(8,128)} %fusion.28.ga_ref, bf16[784,768]{1,0:T(8,128)(2,1)} %get-tuple-element.34.normed_ref), custom_call_target="tpu_custom_call" | custom-call | flops 3699376128 | bytes 25000000 | tf_op jit(solution)/shard_map/pallas_call | solution.py:186
  65.8 3.4 %constant_dynamic-slice_fusion = f32[2,2,2,2,1,96,384]{6,5,4,3,2,1,0:T(8,128)} fusion(f32[2,2,2,2,2,96,384]{6,5,4,3,2,1,0:T(8,128)} %bitcast.85, s32[]{:T(128)S(6)} %select_n.51), kind=kLoop, calls=%fused_computation.67 | loop fusion | bytes 4718596 | tf_op jit(solution)/shard_map/jit(dynamic_index_in_dim)/dynamic_slice | solution.py:287
  69.6 1.6 constant_dynamic-slice_fusion.1
  71.5 0.5 broadcast.108
  72.0 0.7 reduce.3
  72.8 0.9 copy.37
  73.6 0.6 dynamic-slice_bitcast_fusion.2
  74.2 0.6 fusion.18.head_ref
  74.8 9.2 %fusion.29.gn_ref = f32[784,768]{1,0:T(8,128)} fusion(bf16[784,3072]{1,0:T(8,128)(2,1)} %get-tuple-element.38, bf16[3072,768]{1,0:T(8,128)(2,1)} %w_ref.1), kind=kOutput, calls=%fused_computation.90 | convolution fusion | flops 3699376128 | bytes 11943936 | tf_op jit(solution)/shard_map/dot_general | solution.py:526
  84.1 1.9 %bitcast_add_fusion = f32[2,2,2,2,96,384]{5,4,3,2,1,0:T(8,128)S(1)} fusion(f32[2,2,2,2,96,384]{5,4,3,2,1,0:T(8,128)} %bitcast.12, f32[2,2,2,2,2,96,384]{6,5,4,3,2,1,0:T(8,128)S(1)} %bitcast.88, s32[]{:T(128)S(6)} %select_n.50), kind=kLoop, calls=%fused_computation | loop fusion | flops 589824 | bytes 7077892 | tf_op jit(solution)/shard_map/add | solution.py:291
  86.0 2.6 %bitcast_add_fusion.1 = f32[2,2,2,2,96,384]{5,4,3,2,1,0:T(8,128)S(1)} fusion(f32[2,2,2,2,96,384]{5,4,3,2,1,0:T(8,128)} %bitcast.8, f32[2,2,2,2,2,96,384]{6,5,4,3,2,1,0:T(8,128)} %bitcast.83, s32[]{:T(128)S(6)} %select_n.50), kind=kLoop, calls=%fused_computation.1 | loop fusion | flops 589824 | bytes 7077892 | tf_op jit(solution)/shard_map/add | solution.py:291
  88.7 1.8 %collective-permute-start.3 = (bf16[768,384]{1,0:T(8,128)(2,1)S(1)}, bf16[768,384]{1,0:T(8,128)(2,1)}, u32[]{:S(2)}, u32[]{:S(2)}) collective-permute-start(bf16[768,384]{1,0:T(8,128)(2,1)S(1)} %bitcast.94), channel_id=1, source_target_pairs={{0,4},{1,5},{2,6},{3,7},{4,0},{5,1},{6,2},{7,3},{8,12},{9,13},{10,... | collective-permute-start | bytes 1769480 | tf_op jit(solution)/shard_map/ppermute | solution.py:279
  90.6 1.6 collective-permute-start.2
  92.2 15.8 %shard_map.227 = f32[52,768]{1,0:T(8,128)} custom-call(f32[784,768]{1,0:T(8,128)} %fusion.29.gn_ref, f32[784,768]{1,0:T(8,128)} %get-tuple-element.42.hat_ref, f32[784,128]{1,0:T(8,128)} %get-tuple-element.43.rstd_ref, bf16[49,16,768]{2,1,0:T(8,128)(2,1)} %bitcast.92, f32[3,768]{1,0:T(4,128)} %maximum_convert_fusion.vec_ref), custom_call_target="tpu_custom_call" | custom-call | flops 10000000000 | bytes 40000000 | tf_op jit(solution)/shard_map/pallas_call | solution.py:263
  107.9 1.2 convert_add_fusion
  109.3 0.6 collective-permute-start.5
  109.9 0.7 dynamic-slice_convert_fusion.3
  111.0 0.8 reshape.169.sums_ref
  111.8 33.2 %shard_map.228 = (f32[32,2,768]{2,1,0:T(2,128)}, f32[32,16,96]{2,1,0:T(8,128)}, bf16[4,8,16,768]{3,2,1,0:T(8,128)(2,1)}, f32[4,8,2,1024]{3,2,1,0:T(2,128)}) custom-call(f32[32,2,768]{2,1,0:T(2,128)} %reshape.169.sums_ref, f32[32,16,96]{2,1,0:T(8,128)} %bitcast.100, bf16[16,768]{1,0:T(8,128)(2,1)} %copy-done.11, f32[2,1024]{1,0:T(2,128)} %fusion.18.head_ref), custom_call_target="tpu_custom_call" | custom-call | flops 10000000000 | bytes 80000000 | tf_op jit(solution)/shard_map/pallas_call | solution.py:416
  145.1 0.7 copy-done.6
  145.8 1.9 %convert_add_fusion.2 = f32[2,2,96,384]{3,2,1,0:T(8,128)} fusion(bf16[2,2,96,384]{3,2,1,0:T(8,128)(2,1)} %bitcast.99, f32[2,2,2,96,384]{4,3,2,1,0:T(8,128)S(1)} %convert_add_fusion, s32[]{:T(128)S(6)} %select_n.52), kind=kLoop, calls=%fused_computation.11 | loop fusion | flops 294912 | bytes 1474564 | tf_op jit(solution)/shard_map/add | solution.py:291
  147.7 1.0 convert_add_fusion.3
  148.8 0.7 dynamic-slice_convert_fusion.5
  149.4 3.6 %collective-permute-start.6 = (bf16[192,384]{1,0:T(8,128)(2,1)}, bf16[192,384]{1,0:T(8,128)(2,1)S(1)}, u32[]{:S(2)}, u32[]{:S(2)}) collective-permute-start(bf16[192,384]{1,0:T(8,128)(2,1)} %bitcast.27), channel_id=1, source_target_pairs={{0,8},{1,9},{2,10},{3,11},{4,12},{5,13},{6,14},{7,15},{8,0},{9,1},... | collective-permute-start | bytes 442376 | tf_op jit(solution)/shard_map/ppermute | solution.py:279
  153.3 1.7 fusion.4
  155.3 1.0 convolution_add_fusion
  156.4 0.7 slice.52
  157.1 0.6 slice.53
  157.7 0.6 reshape.173
  158.4 0.6 slice_reduce_fusion.1
  159.1 5.8 %collective-permute-done.8 = bf16[192,384]{1,0:T(8,128)(2,1)S(1)} collective-permute-done((bf16[192,384]{1,0:T(8,128)(2,1)S(1)}, bf16[192,384]{1,0:T(8,128)(2,1)S(1)}, u32[]{:S(2)}, u32[]{:S(2)}) %collective-permute-start.8) | collective-permute-done | bytes 147488 | tf_op jit(solution)/shard_map/ppermute | solution.py:279
  165.0 8.0 %collective-permute-done.7 = f32[96,384]{1,0:T(8,128)S(1)} collective-permute-done((f32[96,384]{1,0:T(8,128)S(1)}, f32[96,384]{1,0:T(8,128)S(1)}, u32[]{:S(2)}, u32[]{:S(2)}) %collective-permute-start.7) | collective-permute-done | bytes 147488 | tf_op jit(solution)/shard_map/ppermute | solution.py:279
  173.1 2.3 %collective-permute-done.9 = f32[96,384]{1,0:T(8,128)S(1)} collective-permute-done((f32[96,384]{1,0:T(8,128)S(1)}, f32[96,384]{1,0:T(8,128)S(1)}, u32[]{:S(2)}, u32[]{:S(2)}) %collective-permute-start.9) | collective-permute-done | bytes 147488 | tf_op jit(solution)/shard_map/ppermute | solution.py:279
  175.4 0.7 pad_maximum_fusion
  (118 shorter events, 3.6 us)
Async XLA Ops:
  0.6 45.7 %copy-start = (bf16[768,256]{1,0:T(8,128)(2,1)S(1)}, bf16[768,256]{1,0:T(8,128)(2,1)}, u32[]{:S(2)}) copy-start(bf16[768,256]{1,0:T(8,128)(2,1)} %param.32) | copy-start | bytes 1179652
  4.7 32.7 %slice-start = ((s8[4718592]{0:T(1024)(128)(4,1)}), s8[4194304]{0:T(1024)(128)(4,1)S(1)}, s32[]{:S(2)}) async-start(s8[4718592]{0:T(1024)(128)(4,1)} %bitcast.81), calls=%async_computation | async-start | bytes 8388608
  22.3 15.0 %copy-start.14 = (bf16[768]{0:T(1024)(128)(2,1)S(1)}, bf16[768]{0:T(1024)(128)(2,1)}, u32[]{:S(2)}) copy-start(bf16[768]{0:T(1024)(128)(2,1)} %param.29) | copy-start | bytes 4612
  22.3 15.0 %copy-start.15 = (bf16[768]{0:T(1024)(128)(2,1)S(1)}, bf16[768]{0:T(1024)(128)(2,1)}, u32[]{:S(2)}) copy-start(bf16[768]{0:T(1024)(128)(2,1)} %param.28) | copy-start | bytes 4612
  22.3 15.1 %slice-start.1 = ((s8[4718592]{0:T(1024)(128)(4,1)}), s8[524288]{0:T(1024)(128)(4,1)S(1)}, s32[]{:S(2)}) async-start(s8[4718592]{0:T(1024)(128)(4,1)} %bitcast.81), calls=%async_computation.1 | async-start | bytes 1048576
  37.4 0.9 copy-start.12
  37.4 1.3 copy-start.16
  37.4 1.3 copy-start.17
  37.4 1.3 copy-start.18
  37.4 1.3 copy-start.20
  37.4 1.3 copy-start.21
  37.5 8.8 %copy-start.19 = (bf16[256]{0:T(256)(128)(2,1)S(1)}, bf16[256]{0:T(256)(128)(2,1)}, u32[]{:S(2)}) copy-start(bf16[256]{0:T(256)(128)(2,1)} %param.33) | copy-start | bytes 1540
  48.0 4.4 %copy-start.11 = (bf16[16,768]{1,0:T(8,128)(2,1)}, bf16[16,768]{1,0:T(8,128)(2,1)S(1)}, u32[]{:S(2)}) copy-start(bf16[16,768]{1,0:T(8,128)(2,1)S(1)} %get-tuple-element.73.grad_ref) | copy-start | bytes 73732
  65.8 3.7 %copy-start.2 = (f32[3072,384]{1,0:T(8,128)S(1)}, f32[3072,384]{1,0:T(8,128)}, u32[]{:S(2)}) copy-start(f32[3072,384]{1,0:T(8,128)} %get-tuple-element.39) | copy-start | bytes 14155780
  69.2 14.9 %collective-permute-start.1 = (f32[1536,384]{1,0:T(8,128)}, f32[1536,384]{1,0:T(8,128)}, u32[]{:S(2)}, u32[]{:S(2)}) collective-permute-start(f32[1536,384]{1,0:T(8,128)} %bitcast.11), channel_id=1, source_target_pairs={{0,1},{1,0},{2,3},{3,2},{4,5},{5,4},{6,7},{7,6},{8,9},{9,8},{10,11... | collective-permute-start | bytes 7077896 | tf_op jit(solution)/shard_map/ppermute | solution.py:279
  69.5 1.8 %copy-start.5 = (f32[16,3072]{1,0:T(8,128)S(1)}, f32[16,3072]{1,0:T(8,128)}, u32[]{:S(2)}) copy-start(f32[16,3072]{1,0:T(8,128)} %get-tuple-element.37) | copy-start | bytes 589828
  69.6 2.5 %copy-start.13 = (f32[1,3072]{1,0:T(1,128)S(1)}, f32[1,3072]{1,0:T(1,128)}, u32[]{:S(2)}) copy-start(f32[1,3072]{1,0:T(1,128)} %get-tuple-element.47) | copy-start | bytes 36868
  71.2 14.8 %collective-permute-start = (f32[1536,384]{1,0:T(8,128)}, f32[1536,384]{1,0:T(8,128)}, u32[]{:S(2)}, u32[]{:S(2)}) collective-permute-start(f32[1536,384]{1,0:T(8,128)} %bitcast.7), channel_id=1, source_target_pairs={{0,1},{1,0},{2,3},{3,2},{4,5},{5,4},{6,7},{7,6},{8,9},{9,8},{10,11... | collective-permute-start | bytes 7077896 | tf_op jit(solution)/shard_map/ppermute | solution.py:279
  72.8 11.3 %slice-start.2 = ((s8[4718592]{0:T(1024)(128)(4,1)}), s8[524288]{0:T(1024)(128)(4,1)S(1)}, s32[]{:S(2)}) async-start(s8[4718592]{0:T(1024)(128)(4,1)} %bitcast.86), calls=%async_computation.2 | async-start | bytes 1048576
  74.8 9.2 %slice-start.3 = ((s8[4718592]{0:T(1024)(128)(4,1)}), s8[4194304]{0:T(1024)(128)(4,1)S(1)}, s32[]{:S(2)}) async-start(s8[4718592]{0:T(1024)(128)(4,1)} %bitcast.86), calls=%async_computation.3 | async-start | bytes 8388608
  88.7 19.2 %collective-permute-start.3 = (bf16[768,384]{1,0:T(8,128)(2,1)S(1)}, bf16[768,384]{1,0:T(8,128)(2,1)}, u32[]{:S(2)}, u32[]{:S(2)}) collective-permute-start(bf16[768,384]{1,0:T(8,128)(2,1)S(1)} %bitcast.94), channel_id=1, source_target_pairs={{0,4},{1,5},{2,6},{3,7},{4,0},{5,1},{6,2},{7,3},{8,12},{9,13},{10,... | collective-permute-start | bytes 1769480 | tf_op jit(solution)/shard_map/ppermute | solution.py:279
  90.6 18.5 %collective-permute-start.2 = (bf16[768,384]{1,0:T(8,128)(2,1)S(1)}, bf16[768,384]{1,0:T(8,128)(2,1)S(1)}, u32[]{:S(2)}, u32[]{:S(2)}) collective-permute-start(bf16[768,384]{1,0:T(8,128)(2,1)S(1)} %bitcast.93), channel_id=1, source_target_pairs={{0,2},{1,3},{2,0},{3,1},{4,6},{5,7},{6,4},{7,5},{8,10},{9,11},{10,... | collective-permute-start | bytes 1769480 | tf_op jit(solution)/shard_map/ppermute | solution.py:279
  109.1 1.8 %copy-start.10 = (f32[52,768]{1,0:T(8,128)S(1)}, f32[52,768]{1,0:T(8,128)}, u32[]{:S(2)}) copy-start(f32[52,768]{1,0:T(8,128)} %shard_map.227) | copy-start | bytes 479236
  109.3 35.7 %collective-permute-start.5 = (bf16[384,384]{1,0:T(8,128)(2,1)S(1)}, bf16[384,384]{1,0:T(8,128)(2,1)S(1)}, u32[]{:S(2)}, u32[]{:S(2)}) collective-permute-start(bf16[384,384]{1,0:T(8,128)(2,1)S(1)} %bitcast.98), channel_id=1, source_target_pairs={{0,2},{1,3},{2,0},{3,1},{4,6},{5,7},{6,4},{7,5},{8,10},{9,11},{10,... | collective-permute-start | bytes 884744 | tf_op jit(solution)/shard_map/ppermute | solution.py:279
  110.7 37.0 %collective-permute-start.4 = (bf16[384,384]{1,0:T(8,128)(2,1)}, bf16[384,384]{1,0:T(8,128)(2,1)}, u32[]{:S(2)}, u32[]{:S(2)}) collective-permute-start(bf16[384,384]{1,0:T(8,128)(2,1)} %bitcast.21), channel_id=1, source_target_pairs={{0,4},{1,5},{2,6},{3,7},{4,0},{5,1},{6,2},{7,3},{8,12},{9,13},{10,... | collective-permute-start | bytes 884744 | tf_op jit(solution)/shard_map/ppermute | solution.py:279
  145.0 3.7 %copy-start.8 = (f32[32,16,96]{2,1,0:T(8,128)S(1)}, f32[32,16,96]{2,1,0:T(8,128)}, u32[]{:S(2)}) copy-start(f32[32,16,96]{2,1,0:T(8,128)} %get-tuple-element.56) | copy-start | bytes 589828
  145.0 8.1 %copy-start.7 = (f32[4,8,2,1024]{3,2,1,0:T(2,128)S(1)}, f32[4,8,2,1024]{3,2,1,0:T(2,128)}, u32[]{:S(2)}) copy-start(f32[4,8,2,1024]{3,2,1,0:T(2,128)} %get-tuple-element.59) | copy-start | bytes 786436
  145.0 0.7 copy-start.6
  145.8 9.2 %copy-start.3 = (bf16[4,8,16,768]{3,2,1,0:T(8,128)(2,1)S(1)}, bf16[4,8,16,768]{3,2,1,0:T(8,128)(2,1)}, u32[]{:S(2)}) copy-start(bf16[4,8,16,768]{3,2,1,0:T(8,128)(2,1)} %get-tuple-element.57) | copy-start | bytes 2359300
  148.7 7.5 %copy-start.4 = (f32[2,2,96,384]{3,2,1,0:T(8,128)S(1)}, f32[2,2,96,384]{3,2,1,0:T(8,128)}, u32[]{:S(2)}) copy-start(f32[2,2,96,384]{3,2,1,0:T(8,128)} %convert_add_fusion.2) | copy-start | bytes 1769476
  149.4 6.8 %copy-start.9 = (f32[32,2,768]{2,1,0:T(2,128)S(1)}, f32[32,2,768]{2,1,0:T(2,128)}, u32[]{:S(2)}) copy-start(f32[32,2,768]{2,1,0:T(2,128)} %get-tuple-element.58) | copy-start | bytes 589828
  149.4 9.5 %collective-permute-start.6 = (bf16[192,384]{1,0:T(8,128)(2,1)}, bf16[192,384]{1,0:T(8,128)(2,1)S(1)}, u32[]{:S(2)}, u32[]{:S(2)}) collective-permute-start(bf16[192,384]{1,0:T(8,128)(2,1)} %bitcast.27), channel_id=1, source_target_pairs={{0,8},{1,9},{2,10},{3,11},{4,12},{5,13},{6,14},{7,15},{8,0},{9,1},... | collective-permute-start | bytes 442376 | tf_op jit(solution)/shard_map/ppermute | solution.py:279
  155.3 20.9 %copy-start.1 = (bf16[768,256]{1,0:T(8,128)(2,1)S(1)}, bf16[768,256]{1,0:T(8,128)(2,1)}, u32[]{:S(2)}) copy-start(bf16[768,256]{1,0:T(8,128)(2,1)} %param.32) | copy-start | bytes 1179652
  157.7 7.1 %collective-permute-start.8 = (bf16[192,384]{1,0:T(8,128)(2,1)S(1)}, bf16[192,384]{1,0:T(8,128)(2,1)S(1)}, u32[]{:S(2)}, u32[]{:S(2)}) collective-permute-start(bf16[192,384]{1,0:T(8,128)(2,1)S(1)} %bitcast.103), channel_id=1, source_target_pairs={{0,8},{1,9},{2,10},{3,11},{4,12},{5,13},{6,14},{7,15},{8,0},{9,1},... | collective-permute-start | bytes 442376 | tf_op jit(solution)/shard_map/ppermute | solution.py:279
  159.0 14.0 %collective-permute-start.7 = (f32[96,384]{1,0:T(8,128)S(1)}, f32[96,384]{1,0:T(8,128)S(1)}, u32[]{:S(2)}, u32[]{:S(2)}) collective-permute-start(f32[96,384]{1,0:T(8,128)S(1)} %dynamic-slice_bitcast_fusion.1), channel_id=1, source_target_pairs={{0,16},{1,17},{2,18},{3,19},{4,20},{5,21},{6,22},{7,23},{8,24},{9,... | collective-permute-start | bytes 442376 | tf_op jit(solution)/shard_map/ppermute | solution.py:279
  164.9 10.5 %collective-permute-start.9 = (f32[96,384]{1,0:T(8,128)S(1)}, f32[96,384]{1,0:T(8,128)S(1)}, u32[]{:S(2)}, u32[]{:S(2)}) collective-permute-start(f32[96,384]{1,0:T(8,128)S(1)} %dynamic-slice_bitcast_fusion), channel_id=1, source_target_pairs={{0,16},{1,17},{2,18},{3,19},{4,20},{5,21},{6,22},{7,23},{8,24},{9,... | collective-permute-start | bytes 442376 | tf_op jit(solution)/shard_map/ppermute | solution.py:279
